TPU v7x, 32 devices: a whole 2x2x4 slice. The times are simulated.
32 devices in a mesh: rows: 8 (over z, y), cols: 4 (over x, core).
Axes of the slice: x: 2, y: 2, z: 4, core: 2. Of those that a mesh axis runs over, the one named last changes fastest.
Arguments:
- sketch: float32 [32768, 256], P(('rows', 'cols'))
- tiles: bfloat16 [1280, 512, 512], P(('rows', 'cols')), may hold values from -48 to 48
- tile_user: int32 [1280], P(('rows', 'cols')), may hold values from 0 to 7
- tile_item: int32 [1280], P(('rows', 'cols')), may hold values from 0 to 7
- tile_count: int32 [32], P(('rows', 'cols')), may hold values from 5 to 40, as said below
- item_owner: int32 [4, 8], P('cols'), may hold values from 0 to 7, each once within a row
Outputs:
- projected: float32 [8, 4, 256, 512], P('rows', 'cols')
Inputs may be any that keep to these rules, and one draw needn't show every extreme that they name: `tile_count`: live slots of a device are its first slots; some device has all 40 live in every draw.
All inputs are finite; a program needn't handle non-finite values.
Results may differ from a plain program's by a relative error of at most 0.0029.
Values may be sent and summed in bfloat16 or wider, within the bound.
No kernel may reach another device: no remote copies, remote signals or barrier semaphores. Data moves between devices by JAX's collectives and lax.ppermute only.
A program may use at most 192 MiB of HBM per device.

v0:
```python
import jax
import jax.numpy as jnp
from jax import lax
from jax.sharding import PartitionSpec as P


def accumulate(totals, tile_set, users, items, owner, slab, stop, first_row):
    tile_size = tile_set.shape[1]
    row_count = totals.shape[0]

    def step(index, partial_sums):
        target = owner[items[index]] - first_row
        inside = jnp.logical_and(target >= 0, target < row_count)

        def add_tile(sums):
            basis_rows = lax.dynamic_slice_in_dim(slab, users[index] * tile_size, tile_size, 0)
            partial_value = lax.dot_general(
                basis_rows,
                tile_set[index],
                (((0,), (0,)), ((), ())),
                preferred_element_type=jnp.float32,
            )
            place = jnp.clip(target, 0, row_count - 1)
            current = lax.dynamic_index_in_dim(sums, place, 0, keepdims=False)
            return lax.dynamic_update_index_in_dim(sums, current + partial_value, place, 0)

        return lax.cond(inside, add_tile, lambda sums: sums, partial_sums)

    return lax.fori_loop(0, stop, step, totals)


def body(sketch, tiles, tile_user, tile_item, tile_count, item_owner):
    gram = lax.dot_general(
        sketch,
        sketch,
        (((0,), (0,)), ((), ())),
        precision=lax.Precision.HIGHEST,
        preferred_element_type=jnp.float32,
    )
    total = lax.psum(gram, ("rows", "cols"))
    lower_factor = jnp.linalg.cholesky(total)
    basis_full = lax.linalg.triangular_solve(
        lower_factor, sketch, left_side=False, lower=True, transpose_a=True
    )
    basis = basis_full.astype(jnp.bfloat16)
    slab = lax.all_gather(basis, "cols", axis=0, tiled=True)
    owner = item_owner[0]
    live_count = tile_count[0]
    width = sketch.shape[1]
    tile_size = tiles.shape[2]
    totals = jnp.zeros((owner.shape[0], width, tile_size), jnp.float32)
    totals = accumulate(totals, tiles, tile_user, tile_item, owner, slab, live_count, 0)
    owned = lax.psum_scatter(totals, "rows", scatter_dimension=0, tiled=True)
    return owned[:, None]


def solution(mesh):
    placed = (
        P(("rows", "cols"), None),
        P(("rows", "cols"), None, None),
        P(("rows", "cols")),
        P(("rows", "cols")),
        P(("rows", "cols")),
        P("cols", None),
    )
    return jax.shard_map(
        body, mesh=mesh, in_specs=placed, out_specs=P("rows", "cols", None, None), check_vma=False
    )
```

profile of v0, /device:TPU:2, one launch (start us, length us, event | category | flops | bytes accessed | tf_op | source)
XLA Modules:
  0.0 735.5 jit_solution(1801150780538099880)
XLA Ops:
  6.5 4.1 fusion.14
  10.8 128.2 %all-reduce.3.cloned.1.call-done = f32[256,256]{0,1:T(8,128)} async-done(((f32[256,256]{0,1:T(8,128)}), f32[256,256]{0,1:T(8,128)}) %all-reduce.3.cloned.1.call-update) | async-done | bytes 262160 | tf_op jit(solution)/shard_map/psum | solution.py:40
  139.0 1.1 copy.8
  140.1 1.0 fusion.8
  141.1 11.7 %cholesky.50 = f32[128,128]{1,0:T(8,128)S(1)} custom-call(f32[128,128]{1,0:T(8,128)S(1)} %cholesky.118), custom_call_target="Cholesky" | custom-call | tf_op jit(solution)/shard_map/jit(cholesky)/cholesky | solution.py:41
  152.8 9.8 %custom-call.14 = f32[1,128,128]{1,2,0:T(8,128)S(1)} custom-call(f32[1,128,128]{2,1,0:T(8,128)S(1)} %get-tuple-element.116), custom_call_target="InvertDiagBlocksLowerTriangular" | custom-call | tf_op jit(solution)/shard_map/jit(cholesky)/cholesky | solution.py:41
  163.2 11.7 %cholesky.105 = f32[128,128]{1,0:T(8,128)S(1)} custom-call(f32[128,128]{1,0:T(8,128)S(1)} %convolution_subtract_fusion.1), custom_call_target="Cholesky" | custom-call | tf_op jit(solution)/shard_map/jit(cholesky)/cholesky | solution.py:41
  174.9 0.7 compare_reduce_fusion
  177.0 4.1 while.15
  177.7 1.4 bitcast_dynamic-update-slice_fusion.2
  179.7 1.4 bitcast_dynamic-update-slice_fusion.2
  181.0 19.7 %custom-call.15 = f32[2,128,128]{1,2,0:T(8,128)S(1)} custom-call(f32[2,128,128]{2,1,0:T(8,128)S(1)} %get-tuple-element.78), custom_call_target="InvertDiagBlocksLowerTriangular" | custom-call | tf_op jit(solution)/shard_map/triangular_solve | solution.py:42
  200.7 0.6 fusion.6
  201.4 1.0 convolution_subtract_fusion
  202.4 0.6 convolution_convert_fusion
  203.0 0.8 pad_maximum_fusion
  204.0 20.5 %all-gather.2.cloned.1.call-done = bf16[4096,256]{0,1:T(8,128)(2,1)} async-done(((bf16[1024,256]{0,1:T(8,128)(2,1)}), bf16[4096,256]{0,1:T(8,128)(2,1)}) %all-gather.2.cloned.1.call-update) | async-done | bytes 2097168 | tf_op jit(solution)/shard_map/all_gather | solution.py:46
  224.5 3.3 copy.9
  227.8 2.5 broadcast_in_dim.12
  230.3 51.8 %while.14 = (s32[]{:T(128)}, f32[8,256,512]{2,1,0:T(8,128)}, s32[]{:T(128)}, s32[40]{0:T(128)S(1)}, s32[8]{0:T(128)S(1)}, /*index=5*/s32[40]{0:T(128)S(1)}, bf16...) while((s32[]{:T(128)}, f32[8,256,512]{2,1,0:T(8,128)}, ...), condition=%wide.region_8.9_spmd, body=%wide.region_5.8_spmd.sunk | while | flops 134348832 | bytes 2884007 | solution.py:29
  230.9 0.6 dynamic_slice.28
  233.5 0.6 dynamic_slice.29
  235.4 5.2 conditional.2
  235.4 0.6 dynamic_slice.14
  237.3 1.1 constant_dynamic-slice_fusion
  238.3 2.2 fusion.1
  241.2 0.6 dynamic_slice.28
  243.7 0.6 dynamic_slice.29
  245.6 5.1 conditional.2
  245.6 0.6 dynamic_slice.14
  247.5 1.1 constant_dynamic-slice_fusion
  248.6 2.2 fusion.1
  251.4 0.6 dynamic_slice.28
  254.0 0.6 dynamic_slice.29
  255.8 5.1 conditional.2
  255.9 0.6 dynamic_slice.14
  257.7 1.1 constant_dynamic-slice_fusion
  258.8 2.2 fusion.1
  261.6 0.6 dynamic_slice.28
  266.1 5.1 conditional.2
  266.1 0.6 dynamic_slice.14
  268.0 1.1 constant_dynamic-slice_fusion
  269.0 2.2 fusion.1
  276.3 5.1 conditional.2
  276.3 0.6 dynamic_slice.14
  278.2 1.1 constant_dynamic-slice_fusion
  279.3 2.2 fusion.1
  282.1 446.9 %reduce-scatter.2.cloned.1.call-done = f32[1,256,512]{2,1,0:T(8,128)} async-done(((f32[8,256,512]{2,1,0:T(8,128)}), f32[1,256,512]{2,1,0:T(8,128)}) %reduce-scatter.2.cloned.1.call-update) | async-done | bytes 524304 | tf_op jit(solution)/shard_map/reduce_scatter | solution.py:53
  (32 shorter events, 3.8 us)
Async XLA Ops:
  6.5 194.2 %copy-start = (f32[1024,256]{1,0:T(8,128)S(1)}, f32[1024,256]{1,0:T(8,128)}, u32[]{:S(2)}) copy-start(f32[1024,256]{1,0:T(8,128)} %param.10) | copy-start | bytes 3145732
  6.5 132.5 %all-reduce.3.cloned.1.call-start = ((), (), s32[]{:S(2)}) async-start(), calls=%async_computation.1 | async-start | bytes 524288 | tf_op jit(solution)/shard_map/psum | solution.py:40
  10.7 213.8 %all-gather.2.cloned.1.call-start = ((), (), s32[]{:S(2)}) async-start(), calls=%async_computation.2 | async-start | bytes 2621440 | tf_op jit(solution)/shard_map/all_gather | solution.py:46
  203.9 525.1 %reduce-scatter.2.cloned.1.call-start = ((), (), s32[]{:S(2)}) async-start(), calls=%async_computation.3 | async-start | bytes 4718592 | tf_op jit(solution)/shard_map/reduce_scatter | solution.py:53
  204.0 26.3 %copy-start.1 = (s32[40]{0:T(128)S(1)}, s32[40]{0:T(128)}, u32[]{:S(2)}) copy-start(s32[40]{0:T(128)} %param.13) | copy-start | bytes 484
  204.0 26.3 %copy-start.2 = (s32[1,8]{1,0:T(1,128)S(1)}, s32[1,8]{1,0:T(1,128)}, u32[]{:S(2)}) copy-start(s32[1,8]{1,0:T(1,128)} %param.15) | copy-start | bytes 100
  204.0 26.3 %copy-start.3 = (s32[40]{0:T(128)S(1)}, s32[40]{0:T(128)}, u32[]{:S(2)}) copy-start(s32[40]{0:T(128)} %param.12) | copy-start | bytes 484
Sparse Core Ops, SparseCore 0:
  12.9 126.1 all-reduce.2
  204.0 20.4 all-gather.1
  282.2 446.6 reduce-scatter.1
where the time goes:
time: 744 us; the launch traced here: 736 us
  waiting for transfers between devices  596 us (80%)
  other arithmetic  55.5 us (7%)
  loops' own time  26.9 us (4%)
  local copies, waits for them, and re-layouts  25.1 us (3%)
  matrix products  17.7 us (2%)
  between operations  14.5 us (2%)
    reduce_scatter x1, waiting for transfers between devices, body(): owned = lax.psum_scatter(totals, 'rows', scatter_dimension=0, tiled=True)  447 us
    psum x1, waiting for transfers between devices, body(): total = lax.psum(gram, ('rows', 'cols'))  128 us
    another operation x6, other arithmetic, body(): lower_factor = jnp.linalg.cholesky(total)  34 us
    another operation x5, other arithmetic, body(): lax.linalg.triangular_solve(lower_factor, sketch, left_side=False, lower=...  20.6 us
    all_gather x1, waiting for transfers between devices, body(): slab = lax.all_gather(basis, 'cols', axis=0, tiled=True)  20.5 us
    another operation x1, loops' own time, accumulate(): return lax.fori_loop(0, stop, step, totals)  20.2 us
  transfers between devices with their start and end apart: 3, of which 3 were waited for; matrix products, arithmetic and copies ran while one was open for 0% of the time, Pallas kernels for 0%

commit v1 on v0

v1 whole, which is shorter than its diff:
```python
import functools

import jax
import jax.numpy as jnp
from jax import lax
from jax.experimental import pallas as pl
from jax.experimental.pallas import tpu as pltpu
from jax.sharding import PartitionSpec as P

F32 = jnp.float32
BF16 = jnp.bfloat16
HIGH = lax.Precision.HIGHEST
SLOTS = 6
CHUNKS = 2
NEWTON = 3


def swap(x, axis, count, bit):
    return lax.ppermute(x, axis, [(i, i ^ bit) for i in range(count)])


def places(order, parity):
    found = [parity << order[0]]
    for bit in reversed(order[1:]):
        found = found + [p | (1 << bit) for p in found]
    return found


def tile_kernel(orders, users, items, owner, meta, *refs):
    piece_count = (len(refs) - 1 - 2 * len(orders) - 4)
    pieces = refs[:piece_count]
    tiles = refs[piece_count]
    outs = refs[piece_count + 1 : piece_count + 1 + 2 * len(orders)]
    slab, acc, buf, sems = refs[-4:]
    count, row, col = meta[0], meta[1], meta[2]
    tile_size = tiles.shape[1]
    kc = pieces[0].shape[1]
    per_piece = pieces[0].shape[0] // tile_size

    def fetch(t):
        slot = lax.rem(t, SLOTS)
        return pltpu.make_async_copy(tiles.at[t], buf.at[slot], sems.at[slot])

    for t in range(SLOTS):
        @pl.when(t < count)
        def _():
            fetch(t).start()

    acc[...] = jnp.zeros_like(acc)
    for c in range(piece_count):
        for h in range(per_piece):
            block = pieces[c][h * tile_size : (h + 1) * tile_size, :].T
            high = block.astype(BF16)
            slab[c * per_piece + h, :kc, :] = high
            slab[c * per_piece + h, kc:, :] = (block - high.astype(F32)).astype(BF16)

    def step(t, _):
        user = users[t]
        which = lax.bitwise_xor(user // per_piece, col) * per_piece + lax.rem(user, per_piece)
        place = lax.bitwise_xor(owner[items[t]], row)
        fetch(t).wait()
        both = jnp.dot(slab[which], buf[lax.rem(t, SLOTS)], preferred_element_type=F32)
        acc[place] += both[:kc] + both[kc:]

        @pl.when(t + SLOTS < count)
        def _():
            fetch(t + SLOTS).start()

        return 0

    lax.fori_loop(0, count, step, 0)
    width = tile_size // len(orders)
    for o, order in enumerate(orders):
        cut = slice(o * width, (o + 1) * width)
        for k, place in enumerate(places(order, 0)):
            outs[2 * o][k] = acc[place, :, cut]
        for k, place in enumerate(places(order, 1)):
            outs[2 * o + 1][k] = acc[place, :, cut].astype(BF16)


def tile_sums(orders, row_count, users, items, owner, meta, pieces, tiles):
    kc = pieces[0].shape[1]
    tile_size = tiles.shape[1]
    width = tile_size // len(orders)
    half = row_count // 2
    shapes = []
    for _ in orders:
        shapes.append(jax.ShapeDtypeStruct((half, kc, width), F32))
        shapes.append(jax.ShapeDtypeStruct((half, kc, width), BF16))
    blocks = len(pieces) * pieces[0].shape[0] // tile_size
    smem = pl.BlockSpec(memory_space=pltpu.SMEM)
    vmem = pl.BlockSpec(memory_space=pltpu.VMEM)
    return pl.pallas_call(
        functools.partial(tile_kernel, orders),
        out_shape=shapes,
        in_specs=[smem] * 4 + [vmem] * len(pieces) + [pl.BlockSpec(memory_space=pl.ANY)],
        out_specs=[vmem] * len(shapes),
        scratch_shapes=[
            pltpu.VMEM((blocks, 2 * kc, tile_size), BF16),
            pltpu.VMEM((row_count, kc, tile_size), F32),
            pltpu.VMEM((SLOTS, tile_size, tile_size), BF16),
            pltpu.SemaphoreType.DMA((SLOTS,)),
        ],
        compiler_params=pltpu.CompilerParams(vmem_limit_bytes=48 * 2**20),
        cost_estimate=pl.CostEstimate(
            flops=20 * 4 * kc * tile_size**2, bytes_accessed=20 * 2 * tile_size**2, transcendentals=0
        ),
    )(users, items, owner, meta, *pieces, tiles)


def mm(a, b):
    return lax.dot_general(a, b, (((1,), (0,)), ((), ())), precision=HIGH, preferred_element_type=F32)


def mmt(a, b):
    return lax.dot_general(a, b, (((1,), (1,)), ((), ())), precision=HIGH, preferred_element_type=F32)


def factor_kernel(packed, inverse, check):
    n = packed.shape[1]
    r = lax.broadcasted_iota(jnp.int32, (n, n), 0)
    c = lax.broadcasted_iota(jnp.int32, (n, n), 1)
    mixed = packed[:n]
    flipped = mixed.T
    side = packed[n : 2 * n]
    tail = jnp.broadcast_to(packed[2 * n : 2 * n + 1], (n, n))
    first = jnp.where(r >= c, mixed, flipped)
    second = jnp.where(r < c, mixed, jnp.where(r > c, flipped, tail))
    gram = jnp.concatenate(
        [jnp.concatenate([first, side.T], axis=1), jnp.concatenate([side, second], axis=1)], axis=0
    )
    m = 2 * n
    rr = lax.broadcasted_iota(jnp.int32, (m, m), 0)
    cc = lax.broadcasted_iota(jnp.int32, (m, m), 1)
    on = rr == cc
    eye = jnp.where(on, 1.0, 0.0).astype(F32)
    low = jnp.where(rr > cc, 1.0, jnp.where(on, 0.5, 0.0)).astype(F32)
    diag = jnp.where(on, gram, 0.0)
    scale_row = lax.rsqrt(jnp.sum(diag, axis=0, keepdims=True))
    scale_col = lax.rsqrt(jnp.sum(diag, axis=1, keepdims=True))
    unit = gram * scale_row * scale_col
    off = unit - eye
    spread = jnp.max(jnp.sum(jnp.abs(mm(off, off)), axis=1))
    w = eye - low * off
    for _ in range(NEWTON):
        err = mmt(mm(w, unit), w) - eye
        w = w - mm(low * err, w)
    last = jnp.max(jnp.sum(jnp.abs(err), axis=1))
    inflation = jnp.max(jnp.sum(w * w, axis=0))
    inverse[...] = w * scale_row
    check[0] = spread
    check[1] = last
    check[2] = inflation


def factor(packed):
    n = packed.shape[1]
    return pl.pallas_call(
        factor_kernel,
        out_shape=[jax.ShapeDtypeStruct((2 * n, 2 * n), F32), jax.ShapeDtypeStruct((3,), F32)],
        in_specs=[pl.BlockSpec(memory_space=pltpu.VMEM)],
        out_specs=[pl.BlockSpec(memory_space=pltpu.VMEM), pl.BlockSpec(memory_space=pltpu.SMEM)],
        compiler_params=pltpu.CompilerParams(vmem_limit_bytes=24 * 2**20),
        cost_estimate=pl.CostEstimate(
            flops=11 * 6 * 2 * 8 * n**3, bytes_accessed=6 * 4 * n * n, transcendentals=0
        ),
    )(packed)


def pack(gram):
    n = gram.shape[0] // 2
    r = lax.broadcasted_iota(jnp.int32, (n, n), 0)
    c = lax.broadcasted_iota(jnp.int32, (n, n), 1)
    mixed = jnp.where(r >= c, gram[:n, :n], gram[n:, n:])
    tail = jnp.sum(jnp.where(r == c, gram[n:, n:], 0.0), axis=0, keepdims=True)
    return jnp.concatenate([mixed, gram[n:, :n], jnp.broadcast_to(tail, (8, n))], axis=0)


def full_path(sketch, tiles, tile_user, tile_item, tile_count, item_owner, packed):
    n = packed.shape[1]
    r = lax.broadcasted_iota(jnp.int32, (n, n), 0)
    c = lax.broadcasted_iota(jnp.int32, (n, n), 1)
    mixed, side, tail = packed[:n], packed[n : 2 * n], packed[2 * n : 2 * n + 1]
    first = jnp.where(r >= c, mixed, mixed.T)
    second = jnp.where(r < c, mixed, jnp.where(r > c, mixed.T, tail))
    gram = jnp.block([[first, side.T], [side, second]])
    lower = jnp.linalg.cholesky(gram)
    basis = lax.linalg.triangular_solve(lower, sketch, left_side=False, lower=True, transpose_a=True).astype(BF16)
    slab = lax.all_gather(basis, "cols", axis=0, tiled=True)
    owner = item_owner[0]
    tile_size = tiles.shape[2]

    def step(index, sums):
        rows = lax.dynamic_slice_in_dim(slab, tile_user[index] * tile_size, tile_size, 0)
        part = lax.dot_general(rows, tiles[index], (((0,), (0,)), ((), ())), preferred_element_type=F32)
        place = owner[tile_item[index]]
        now = lax.dynamic_index_in_dim(sums, place, 0, keepdims=False)
        return lax.dynamic_update_index_in_dim(sums, now + part, place, 0)

    totals = jnp.zeros((owner.shape[0], sketch.shape[1], tile_size), F32)
    totals = lax.fori_loop(0, tile_count[0], step, totals)
    return lax.psum_scatter(totals, "rows", scatter_dimension=0, tiled=True)[0]


def body(rows, cols, sketch, tiles, tile_user, tile_item, tile_count, item_owner):
    width = sketch.shape[1]
    row_bits = rows.bit_length() - 1
    first_order = tuple(range(row_bits))
    orders = (first_order, (1, 0) + first_order[2:])
    row = lax.axis_index("rows")
    col = lax.axis_index("cols")
    meta = jnp.stack([tile_count[0], row, col]).astype(jnp.int32)
    owner = item_owner[0]

    kc = width // CHUNKS
    gathered = []
    for k in range(CHUNKS):
        pieces = [sketch[:, k * kc : (k + 1) * kc]]
        gathered.append(pieces)
    bits = []
    bit = cols // 2
    while bit:
        bits.append(bit)
        bit //= 2
    for k in range(CHUNKS):
        have = {0: gathered[k][0]}
        for bit in bits:
            for place in list(have):
                have[place | bit] = swap(have[place], "cols", cols, bit)
        gathered[k] = [have[i] for i in range(cols)]

    gram = lax.dot_general(
        sketch, sketch, (((0,), (0,)), ((), ())), precision=HIGH, preferred_element_type=F32
    )
    packed = pack(gram)
    for bit in reversed(bits):
        packed = packed + swap(packed, "cols", cols, bit)
    for b in range(row_bits):
        packed = packed + swap(packed, "rows", rows, 1 << b)
    inverse, check = factor(packed)

    halves = []
    for k in range(CHUNKS):
        outs = tile_sums(orders, rows, tile_user, tile_item, owner, meta, gathered[k], tiles)
        done = []
        for o, order in enumerate(orders):
            keep, send = outs[2 * o], outs[2 * o + 1]
            for pos, b in enumerate(order):
                got = swap(send, "rows", rows, 1 << b)
                total = keep + got.astype(F32)
                if pos + 1 < len(order):
                    half = total.shape[0] // 2
                    keep, send = total[:half], total[half:].astype(BF16)
            done.append(total[0])
        halves.append(jnp.concatenate(done, axis=1))
    sums = jnp.concatenate(halves, axis=0)
    good = (check[0] < 0.16) & (check[1] < 1e-3) & (check[2] < 1.1)
    out = lax.cond(
        good,
        lambda: mm(inverse, sums),
        lambda: full_path(sketch, tiles, tile_user, tile_item, tile_count, item_owner, packed),
    )
    return out[None, None]


def solution(mesh):
    placed = (
        P(("rows", "cols"), None),
        P(("rows", "cols"), None, None),
        P(("rows", "cols")),
        P(("rows", "cols")),
        P(("rows", "cols")),
        P("cols", None),
    )
    return jax.shard_map(
        functools.partial(body, mesh.shape["rows"], mesh.shape["cols"]),
        mesh=mesh,
        in_specs=placed,
        out_specs=P("rows", "cols", None, None),
        check_vma=False,
    )
```

time: 744 us -> 712 us (0.957)
  waiting for transfers between devices: 596 us -> 148 us
  loops' own time: 26.9 us -> 211 us
  local copies, waits for them, and re-layouts: 25.1 us -> 123 us
  matrix products: 17.7 us -> 95.7 us
  Pallas kernels: 0 us -> 34.9 us
  starting transfers between devices: 0.09 us -> 20.1 us
    reduce_scatter x1, waiting for transfers between devices: 447 us -> 89.8 us  [full_path(): return lax.psum_scatter(totals, 'rows', scatter_dimension=0, tiled=True)[0]]
    another operation x7 -> x3, loops' own time: 26.9 us -> 211 us  [the longest x1 209 us: full_path(): totals = lax.fori_loop(0, tile_count[0], step, totals)]
    psum x1 -> x0, waiting for transfers between devices: 128 us -> none  [body(): total = lax.psum(gram, ('rows', 'cols'))]
    dynamic_slice x20 -> x160, local copies, waits for them, and re-layouts: 14.2 us -> 114 us  [the longest x80 47 us: step(): place = owner[tile_item[index]]]
    dot_general x6 -> x41, matrix products: 15 us -> 92.9 us  [the longest x40 89.6 us: step(): lax.dot_general(rows, tiles[index], (((0,), (0,)), ((), ())), preferred_e...]
    ppermute x0 -> x23, waiting for transfers between devices: none -> 37.6 us  [swap(): return lax.ppermute(x, axis, [(i, i ^ bit) for i in range(count)])]
    pallas_call x0 -> x3, Pallas kernels: none -> 34.9 us  [the longest x2 29.6 us: tile_sums(): pl.pallas_call(functools.partial(tile_kernel, orders), out_shape=shapes,...]
    ppermute x0 -> x23, starting transfers between devices: none -> 19.8 us  [swap(): return lax.ppermute(x, axis, [(i, i ^ bit) for i in range(count)])]
  transfers between devices with their start and end apart: 3 -> 25, of which waited for: 3 -> 13; matrix products, arithmetic and copies ran while one was open for 0% -> 0% of each run, Pallas kernels for 0% -> 5%
where the time goes in v1:
time: 712 us; the launch traced here: 704 us
  loops' own time  211 us (30%)
  waiting for transfers between devices  148 us (21%)
  local copies, waits for them, and re-layouts  123 us (17%)
  matrix products  95.7 us (13%)
  other arithmetic  55.6 us (8%)
  Pallas kernels  34.9 us (5%)
  starting transfers between devices  20.1 us (3%)
  between operations  16.3 us (2%)
    another operation x1, loops' own time, full_path(): totals = lax.fori_loop(0, tile_count[0], step, totals)  209 us
    reduce_scatter x1, waiting for transfers between devices, full_path(): return lax.psum_scatter(totals, 'rows', scatter_dimension=0, tiled=True)[0]  89.8 us
    dot_general x40, matrix products, step(): lax.dot_general(rows, tiles[index], (((0,), (0,)), ((), ())), preferred_e...  89.6 us
    dynamic_slice x80, local copies, waits for them, and re-layouts, step(): place = owner[tile_item[index]]  47 us
    dynamic_slice x40, local copies, waits for them, and re-layouts, step(): now = lax.dynamic_index_in_dim(sums, place, 0, keepdims=False)  43.3 us
    ppermute x23, waiting for transfers between devices, swap(): return lax.ppermute(x, axis, [(i, i ^ bit) for i in range(count)])  37.6 us
    another operation x6, other arithmetic, full_path(): lower = jnp.linalg.cholesky(gram)  34.2 us
    pallas_call x2, Pallas kernels, tile_sums(): pl.pallas_call(functools.partial(tile_kernel, orders), out_shape=shapes,...  29.6 us
  transfers between devices with their start and end apart: 25, of which 13 were waited for; matrix products, arithmetic and copies ran while one was open for 0% of the time, Pallas kernels for 5%

profile of v1, /device:TPU:2, one launch (start us, length us, event | category | flops | bytes accessed | tf_op | source)
XLA Modules:
  0.0 704.3 jit_solution(11321562046421282384)
XLA Ops:
  6.5 3.4 fusion.22
  13.6 15.4 %collective-permute-done.1 = f32[264,128]{1,0:T(8,128)S(1)} collective-permute-done((f32[264,128]{1,0:T(8,128)S(1)}, f32[264,128]{1,0:T(8,128)S(1)}, u32[]{:S(2)}, u32[]{:S(2)}) %collective-permute-start.1) | collective-permute-done | bytes 135200 | tf_op jit(solution)/shard_map/ppermute | solution.py:19
  31.1 3.0 collective-permute-done.2
  35.8 3.4 collective-permute-done.3
  39.2 2.7 collective-permute-start.4
  43.1 3.5 collective-permute-done.4
  46.7 5.2 shard_map.66
  52.0 15.0 %shard_map.67 = (f32[4,128,256]{2,1,0:T(8,128)S(1)}, bf16[4,128,256]{2,1,0:T(8,128)(2,1)S(1)}, f32[4,128,256]{2,1,0:T(8,128)S(1)}, bf16[4,128,256]{2,1,0:T(8,128)(2,1)S(1)}) custom-call(s32[40]{0:T(128)S(1)} %copy-done.3, s32[40]{0:T(128)S(1)} %copy-done.2, s32[8]{0:T(128)S(1)} %bitcast.87, s32[3]{0:T(128)S(1)} %pad_add_fusion.meta, ...), custom_call_target="tpu_custom_call" | custom-call | flops 2684354560 | bytes 10485760 | tf_op jit(solution)/shard_map/pallas_call | solution.py:93
  69.7 14.6 %shard_map.68 = (f32[4,128,256]{2,1,0:T(8,128)S(1)}, bf16[4,128,256]{2,1,0:T(8,128)(2,1)S(1)}, f32[4,128,256]{2,1,0:T(8,128)S(1)}, bf16[4,128,256]{2,1,0:T(8,128)(2,1)S(1)}) custom-call(s32[40]{0:T(128)S(1)} %copy-done.3, s32[40]{0:T(128)S(1)} %copy-done.2, s32[8]{0:T(128)S(1)} %bitcast.88, s32[3]{0:T(128)S(1)} %pad_add_fusion.meta, ...), custom_call_target="tpu_custom_call" | custom-call | flops 2684354560 | bytes 10485760 | tf_op jit(solution)/shard_map/pallas_call | solution.py:93
  88.8 3.4 collective-permute-done.17
  96.3 3.0 collective-permute-start.13
  99.4 3.0 collective-permute-start.22
  103.7 2.7 collective-permute-done.13
  107.8 589.7 %conditional.1 = (f32[1,1,256,512]{3,2,1,0:T(8,128)}) conditional(s32[]{:T(128)} %bitcast.19, (s32[1]{0:T(128)}, f32[264,128]{1,0:T(8,128)S(1)}, f32[1024,256]{1,0:T(8,128)S(1)}, s32[1,8]{1,0:T(1,128)S(1)}, s32[40]{0:T(128)S(1)}, /*index=5*/s32[40]{0:T(128)S(1)}, bf16[40,512,512]{2,1,0:T(8,128)(2,1)}) %tuple.70, (f32[256,256]{1,0:T(8,128)S(1)}, ...), branch_computations={%region_1.9_spmd, %region_9.10_spmd} | conditional | flops 791134464 | bytes 39858424 | solution.py:258
  108.8 11.7 %cholesky.8 = f32[128,128]{1,0:T(8,128)S(1)} custom-call(f32[128,128]{1,0:T(8,128)S(1)} %cholesky.47), custom_call_target="Cholesky" | custom-call | tf_op jit(solution)/shard_map/cond/branch_0_fun/jit(cholesky)/cholesky | solution.py:187
  120.8 9.8 %custom-call.12 = f32[1,128,128]{1,2,0:T(8,128)S(1)} custom-call(f32[1,128,128]{2,1,0:T(8,128)S(1)} %copy.15), custom_call_target="InvertDiagBlocksLowerTriangular" | custom-call | tf_op jit(solution)/shard_map/cond/branch_0_fun/jit(cholesky)/cholesky | solution.py:187
  131.1 11.7 %cholesky.30 = f32[128,128]{1,0:T(8,128)S(1)} custom-call(f32[128,128]{1,0:T(8,128)S(1)} %convolution_subtract_fusion.1), custom_call_target="Cholesky" | custom-call | tf_op jit(solution)/shard_map/cond/branch_0_fun/jit(cholesky)/cholesky | solution.py:187
  145.1 4.0 while.11
  149.1 19.7 %custom-call.13 = f32[2,128,128]{1,2,0:T(8,128)S(1)} custom-call(f32[2,128,128]{2,1,0:T(8,128)S(1)} %get-tuple-element.107), custom_call_target="InvertDiagBlocksLowerTriangular" | custom-call | tf_op jit(solution)/shard_map/cond/branch_0_fun/triangular_solve | solution.py:188
  172.0 20.5 %all-gather.2.cloned.1.call-done = bf16[4096,256]{0,1:T(8,128)(2,1)} async-done(((bf16[1024,256]{0,1:T(8,128)(2,1)}), bf16[4096,256]{0,1:T(8,128)(2,1)}) %all-gather.2.cloned.1.call-update) | async-done | bytes 2097168 | tf_op jit(solution)/shard_map/cond/branch_0_fun/all_gather | solution.py:189
  192.5 2.5 broadcast.95
  195.0 412.7 %while.10 = (s32[]{:T(128)}, f32[8,256,512]{2,1,0:T(8,128)}, s32[]{:T(128)}, s32[40]{0:T(128)S(1)}, s32[8]{0:T(128)S(1)}, /*index=5*/s32[40]{0:T(128)S(1)}, bf16...) while((s32[]{:T(128)}, f32[8,256,512]{2,1,0:T(8,128)}, ...), condition=%wide.region_7.7_spmd, body=%wide.region_6.6_spmd.sunk | while | flops 134348816 | bytes 2883925 | solution.py:201
  203.0 2.2 fusion.37
  213.3 2.2 fusion.37
  223.7 2.2 fusion.37
  254.5 2.2 fusion.37
  264.9 2.2 fusion.37
  275.2 2.2 fusion.37
  285.5 2.2 fusion.37
  306.1 2.2 fusion.37
  316.4 2.2 fusion.37
  326.7 2.2 fusion.37
  347.3 2.2 fusion.37
  378.2 2.2 fusion.37
  398.8 2.2 fusion.37
  409.1 2.2 fusion.37
  450.3 2.2 fusion.37
  470.9 2.2 fusion.37
  481.2 2.2 fusion.37
  491.5 2.2 fusion.37
  501.8 2.2 fusion.37
  522.4 2.2 fusion.37
  543.0 2.3 fusion.37
  553.3 2.2 fusion.37
  563.6 2.2 fusion.37
  573.9 2.3 fusion.37
  594.5 2.2 fusion.37
  607.7 89.8 %reduce-scatter.2.cloned.1.call-done = f32[1,256,512]{2,1,0:T(8,128)} async-done(((f32[8,256,512]{2,1,0:T(8,128)}), f32[1,256,512]{2,1,0:T(8,128)}) %reduce-scatter.2.cloned.1.call-update) | async-done | bytes 524304 | tf_op jit(solution)/shard_map/cond/branch_0_fun/reduce_scatter | solution.py:202
  (292 shorter events, 177.1 us)
Async XLA Ops:
  10.0 1.4 collective-permute-start
  11.3 19.3 %collective-permute-start.6 = (f32[1024,128]{1,0:T(8,128)S(1)}, f32[1024,128]{1,0:T(8,128)S(1)}, u32[]{:S(2)}, u32[]{:S(2)}) collective-permute-start(f32[1024,128]{1,0:T(8,128)S(1)} %get-tuple-element.152.refs_0_), channel_id=1, source_target_pairs={{0,2},{1,3},{2,0},{3,1},{4,6},{5,7},{6,4},{7,5},{8,10},{9,11},{10,... | collective-permute-start | bytes 1572872 | tf_op jit(solution)/shard_map/ppermute | solution.py:19
  11.4 17.6 %collective-permute-start.1 = (f32[264,128]{1,0:T(8,128)S(1)}, f32[264,128]{1,0:T(8,128)S(1)}, u32[]{:S(2)}, u32[]{:S(2)}) collective-permute-start(f32[264,128]{1,0:T(8,128)S(1)} %fusion.18), channel_id=1, source_target_pairs={{0,2},{1,3},{2,0},{3,1},{4,6},{5,7},{6,4},{7,5},{8,10},{9,11},{10,... | collective-permute-start | bytes 405512 | tf_op jit(solution)/shard_map/ppermute | solution.py:19
  13.5 29.1 %collective-permute-start.15 = (f32[1024,128]{1,0:T(8,128)S(1)}, f32[1024,128]{1,0:T(8,128)S(1)}, u32[]{:S(2)}, u32[]{:S(2)}) collective-permute-start(f32[1024,128]{1,0:T(8,128)S(1)} %get-tuple-element.153.refs_0_), channel_id=1, source_target_pairs={{0,2},{1,3},{2,0},{3,1},{4,6},{5,7},{6,4},{7,5},{8,10},{9,11},{10,... | collective-permute-start | bytes 1572872 | tf_op jit(solution)/shard_map/ppermute | solution.py:19
  29.0 5.1 collective-permute-start.2
  30.6 21.3 %collective-permute-start.5 = (f32[1024,128]{1,0:T(8,128)S(1)}, f32[1024,128]{1,0:T(8,128)S(1)}, u32[]{:S(2)}, u32[]{:S(2)}) collective-permute-start(f32[1024,128]{1,0:T(8,128)S(1)} %get-tuple-element.152.refs_0_), channel_id=1, source_target_pairs={{0,1},{1,0},{2,3},{3,2},{4,5},{5,4},{6,7},{7,6},{8,9},{9,8},{10,11... | collective-permute-start | bytes 1572872 | tf_op jit(solution)/shard_map/ppermute | solution.py:19
  30.6 21.3 %collective-permute-start.7 = (f32[1024,128]{1,0:T(8,128)S(1)}, f32[1024,128]{1,0:T(8,128)}, u32[]{:S(2)}, u32[]{:S(2)}) collective-permute-start(f32[1024,128]{1,0:T(8,128)S(1)} %collective-permute-done.6.refs_2_), channel_id=1, source_target_pairs={{0,1},{1,0},{2,3},{3,2},{4,5},{5,4},{6,7},{7,6},{8,9},{9,8},{10,11... | collective-permute-start | bytes 1572872 | tf_op jit(solution)/shard_map/ppermute | solution.py:19
  34.1 5.1 collective-permute-start.3
  39.2 7.4 %collective-permute-start.4 = (f32[264,128]{1,0:T(8,128)S(1)}, f32[264,128]{1,0:T(8,128)S(1)}, u32[]{:S(2)}, u32[]{:S(2)}) collective-permute-start(f32[264,128]{1,0:T(8,128)S(1)} %add.101), channel_id=1, source_target_pairs={{0,16},{4,20},{8,24},{12,28},{16,0},{20,4},{24,8},{28,12},{1,17},{... | collective-permute-start | bytes 405512 | tf_op jit(solution)/shard_map/ppermute | solution.py:19
  41.9 27.8 %collective-permute-start.14 = (f32[1024,128]{1,0:T(8,128)S(1)}, f32[1024,128]{1,0:T(8,128)S(1)}, u32[]{:S(2)}, u32[]{:S(2)}) collective-permute-start(f32[1024,128]{1,0:T(8,128)S(1)} %get-tuple-element.153.refs_0_), channel_id=1, source_target_pairs={{0,1},{1,0},{2,3},{3,2},{4,5},{5,4},{6,7},{7,6},{8,9},{9,8},{10,11... | collective-permute-start | bytes 1572872 | tf_op jit(solution)/shard_map/ppermute | solution.py:19
  42.6 27.1 %collective-permute-start.16 = (f32[1024,128]{1,0:T(8,128)S(1)}, f32[1024,128]{1,0:T(8,128)S(1)}, u32[]{:S(2)}, u32[]{:S(2)}) collective-permute-start(f32[1024,128]{1,0:T(8,128)S(1)} %collective-permute-done.15.refs_2_), channel_id=1, source_target_pairs={{0,1},{1,0},{2,3},{3,2},{4,5},{5,4},{6,7},{7,6},{8,9},{9,8},{10,11... | collective-permute-start | bytes 1572872 | tf_op jit(solution)/shard_map/ppermute | solution.py:19
  46.7 5.3 copy-start.1
  46.7 5.3 copy-start.2
  46.7 5.3 copy-start.3
  67.0 17.5 %collective-permute-start.8 = (bf16[4,128,256]{2,1,0:T(8,128)(2,1)S(1)}, bf16[4,128,256]{2,1,0:T(8,128)(2,1)S(1)}, u32[]{:S(2)}, u32[]{:S(2)}) collective-permute-start(bf16[4,128,256]{2,1,0:T(8,128)(2,1)S(1)} %get-tuple-element.92), channel_id=1, source_target_pairs={{0,4},{4,0},{8,12},{12,8},{16,20},{20,16},{24,28},{28,24},{1,5},{5... | collective-permute-start | bytes 786440 | tf_op jit(solution)/shard_map/ppermute | solution.py:19
  69.6 17.1 %collective-permute-start.11 = (bf16[4,128,256]{2,1,0:T(8,128)(2,1)S(1)}, bf16[4,128,256]{2,1,0:T(8,128)(2,1)S(1)}, u32[]{:S(2)}, u32[]{:S(2)}) collective-permute-start(bf16[4,128,256]{2,1,0:T(8,128)(2,1)S(1)} %get-tuple-element.94), channel_id=1, source_target_pairs={{0,8},{4,12},{8,0},{12,4},{16,24},{20,28},{24,16},{28,20},{1,9},{5... | collective-permute-start | bytes 786440 | tf_op jit(solution)/shard_map/ppermute | solution.py:19
  84.4 7.8 %collective-permute-start.17 = (bf16[4,128,256]{2,1,0:T(8,128)(2,1)S(1)}, bf16[4,128,256]{2,1,0:T(8,128)(2,1)S(1)}, u32[]{:S(2)}, u32[]{:S(2)}) collective-permute-start(bf16[4,128,256]{2,1,0:T(8,128)(2,1)S(1)} %get-tuple-element.96), channel_id=1, source_target_pairs={{0,4},{4,0},{8,12},{12,8},{16,20},{20,16},{24,28},{28,24},{1,5},{5... | collective-permute-start | bytes 786440 | tf_op jit(solution)/shard_map/ppermute | solution.py:19
  84.4 9.3 %collective-permute-start.20 = (bf16[4,128,256]{2,1,0:T(8,128)(2,1)S(1)}, bf16[4,128,256]{2,1,0:T(8,128)(2,1)S(1)}, u32[]{:S(2)}, u32[]{:S(2)}) collective-permute-start(bf16[4,128,256]{2,1,0:T(8,128)(2,1)S(1)} %get-tuple-element.98), channel_id=1, source_target_pairs={{0,8},{4,12},{8,0},{12,4},{16,24},{20,28},{24,16},{28,20},{1,9},{5... | collective-permute-start | bytes 786440 | tf_op jit(solution)/shard_map/ppermute | solution.py:19
  84.6 11.5 %collective-permute-start.9 = (bf16[2,128,256]{2,1,0:T(8,128)(2,1)S(1)}, bf16[2,128,256]{2,1,0:T(8,128)(2,1)S(1)}, u32[]{:S(2)}, u32[]{:S(2)}) collective-permute-start(bf16[2,128,256]{2,1,0:T(8,128)(2,1)S(1)} %slice.221), channel_id=1, source_target_pairs={{0,8},{4,12},{8,0},{12,4},{16,24},{20,28},{24,16},{28,20},{1,9},{5... | collective-permute-start | bytes 393224 | tf_op jit(solution)/shard_map/ppermute | solution.py:19
  86.8 9.4 %collective-permute-start.12 = (bf16[2,128,256]{2,1,0:T(8,128)(2,1)S(1)}, bf16[2,128,256]{2,1,0:T(8,128)(2,1)S(1)}, u32[]{:S(2)}, u32[]{:S(2)}) collective-permute-start(bf16[2,128,256]{2,1,0:T(8,128)(2,1)S(1)} %slice.220), channel_id=1, source_target_pairs={{0,4},{4,0},{8,12},{12,8},{16,20},{20,16},{24,28},{28,24},{1,5},{5... | collective-permute-start | bytes 393224 | tf_op jit(solution)/shard_map/ppermute | solution.py:19
  92.2 15.6 %copy-start = (f32[1024,256]{1,0:T(8,128)S(1)}, f32[1024,256]{1,0:T(8,128)}, u32[]{:S(2)}) copy-start(f32[1024,256]{1,0:T(8,128)} %param.10) | copy-start | bytes 3145732
  92.3 6.9 collective-permute-start.18
  93.8 5.5 collective-permute-start.21
  96.1 7.5 %collective-permute-start.10 = (bf16[1,128,256]{2,1,0:T(8,128)(2,1)S(1)}, bf16[1,128,256]{2,1,0:T(8,128)(2,1)S(1)}, u32[]{:S(2)}, u32[]{:S(2)}) collective-permute-start(bf16[1,128,256]{2,1,0:T(8,128)(2,1)S(1)} %slice.225), channel_id=1, source_target_pairs={{0,16},{4,20},{8,24},{12,28},{16,0},{20,4},{24,8},{28,12},{1,17},{... | collective-permute-start | bytes 196616 | tf_op jit(solution)/shard_map/ppermute | solution.py:19
  96.3 10.1 %collective-permute-start.13 = (bf16[1,128,256]{2,1,0:T(8,128)(2,1)S(1)}, bf16[1,128,256]{2,1,0:T(8,128)(2,1)S(1)}, u32[]{:S(2)}, u32[]{:S(2)}) collective-permute-start(bf16[1,128,256]{2,1,0:T(8,128)(2,1)S(1)} %slice.224), channel_id=1, source_target_pairs={{0,16},{4,20},{8,24},{12,28},{16,0},{20,4},{24,8},{28,12},{1,17},{... | collective-permute-start | bytes 196616 | tf_op jit(solution)/shard_map/ppermute | solution.py:19
  99.3 7.8 %collective-permute-start.19 = (bf16[1,128,256]{2,1,0:T(8,128)(2,1)S(1)}, bf16[1,128,256]{2,1,0:T(8,128)(2,1)S(1)}, u32[]{:S(2)}, u32[]{:S(2)}) collective-permute-start(bf16[1,128,256]{2,1,0:T(8,128)(2,1)S(1)} %slice.223), channel_id=1, source_target_pairs={{0,16},{4,20},{8,24},{12,28},{16,0},{20,4},{24,8},{28,12},{1,17},{... | collective-permute-start | bytes 196616 | tf_op jit(solution)/shard_map/ppermute | solution.py:19
  99.4 8.3 %collective-permute-start.22 = (bf16[1,128,256]{2,1,0:T(8,128)(2,1)S(1)}, bf16[1,128,256]{2,1,0:T(8,128)(2,1)S(1)}, u32[]{:S(2)}, u32[]{:S(2)}) collective-permute-start(bf16[1,128,256]{2,1,0:T(8,128)(2,1)S(1)} %slice.222), channel_id=1, source_target_pairs={{0,16},{4,20},{8,24},{12,28},{16,0},{20,4},{24,8},{28,12},{1,17},{... | collective-permute-start | bytes 196616 | tf_op jit(solution)/shard_map/ppermute | solution.py:19
  107.8 84.6 %all-gather.2.cloned.1.call-start = ((), (), s32[]{:S(2)}) async-start(), calls=%async_computation.1 | async-start | bytes 2621440 | tf_op jit(solution)/shard_map/cond/branch_0_fun/all_gather | solution.py:189
  172.0 525.5 %reduce-scatter.2.cloned.1.call-start = ((), (), s32[]{:S(2)}) async-start(), calls=%async_computation.2 | async-start | bytes 4718592 | tf_op jit(solution)/shard_map/cond/branch_0_fun/reduce_scatter | solution.py:202
Sparse Core Ops, SparseCore 0:
  172.1 20.3 all-gather.1
  607.9 89.5 reduce-scatter.1

commit v2 on v1

--- a/solution.py
+++ b/solution.py
@@ -12,7 +12,7 @@
 HIGH = lax.Precision.HIGHEST
 SLOTS = 6
 CHUNKS = 2
-NEWTON = 3
+NEWTON = 2
 
 
 def swap(x, axis, count, bit):
@@ -140,7 +140,8 @@
     scale_col = lax.rsqrt(jnp.sum(diag, axis=1, keepdims=True))
     unit = gram * scale_row * scale_col
     off = unit - eye
-    spread = jnp.max(jnp.sum(jnp.abs(mm(off, off)), axis=1))
+    square = jnp.dot(off, off, preferred_element_type=F32)
+    spread = jnp.max(jnp.sum(jnp.abs(jnp.dot(square, square, preferred_element_type=F32)), axis=1))
     w = eye - low * off
     for _ in range(NEWTON):
         err = mmt(mm(w, unit), w) - eye
@@ -254,7 +255,7 @@
             done.append(total[0])
         halves.append(jnp.concatenate(done, axis=1))
     sums = jnp.concatenate(halves, axis=0)
-    good = (check[0] < 0.16) & (check[1] < 1e-3) & (check[2] < 1.1)
+    good = (check[0] < 0.025) & (check[1] < 0.01) & (check[2] < 1.1)
     out = lax.cond(
         good,
         lambda: mm(inverse, sums),

time: 712 us -> 710 us (level)
  waiting for transfers between devices: 148 us -> 510 us
  loops' own time: 211 us -> 33.6 us
  local copies, waits for them, and re-layouts: 123 us -> 26.2 us
  matrix products: 95.7 us -> 19.5 us
  Pallas kernels: 34.9 us -> 12.6 us
  starting transfers between devices: 20.1 us -> 28.3 us
    reduce_scatter x1, waiting for transfers between devices: 89.8 us -> 440 us  [full_path(): return lax.psum_scatter(totals, 'rows', scatter_dimension=0, tiled=True)[0]]
    another operation x1, loops' own time: 209 us -> 31.9 us  [full_path(): totals = lax.fori_loop(0, tile_count[0], step, totals)]
    dot_general x40 -> x6, matrix products: 89.6 us -> 13.4 us  [step(): lax.dot_general(rows, tiles[index], (((0,), (0,)), ((), ())), preferred_e...]
    dynamic_slice x80 -> x12, local copies, waits for them, and re-layouts: 47 us -> 7.05 us  [step(): place = owner[tile_item[index]]]
    dynamic_slice x40 -> x6, local copies, waits for them, and re-layouts: 43.3 us -> 6.5 us  [step(): now = lax.dynamic_index_in_dim(sums, place, 0, keepdims=False)]
    pallas_call x2, Pallas kernels: 29.6 us -> 8.69 us  [tile_sums(): pl.pallas_call(functools.partial(tile_kernel, orders), out_shape=shapes,...]
    dynamic_slice x40 -> x6, local copies, waits for them, and re-layouts: 23.6 us -> 3.53 us  [step(): tile_user[index] * tile_size]
    all_gather x1, waiting for transfers between devices: 20.5 us -> 35.9 us  [full_path(): slab = lax.all_gather(basis, 'cols', axis=0, tiled=True)]
  transfers between devices with their start and end apart: 25 -> 25, of which waited for: 13 -> 12; matrix products, arithmetic and copies ran while one was open for 0% -> 0% of each run, Pallas kernels for 5% -> 2%
where the time goes in v2:
time: 710 us; the launch traced here: 702 us
  waiting for transfers between devices  510 us (72%)
  other arithmetic  55.6 us (8%)
  loops' own time  33.6 us (5%)
  starting transfers between devices  28.3 us (4%)
  local copies, waits for them, and re-layouts  26.2 us (4%)
  matrix products  19.5 us (3%)
  between operations  16.2 us (2%)
  Pallas kernels  12.6 us (2%)
    reduce_scatter x1, waiting for transfers between devices, full_path(): return lax.psum_scatter(totals, 'rows', scatter_dimension=0, tiled=True)[0]  440 us
    all_gather x1, waiting for transfers between devices, full_path(): slab = lax.all_gather(basis, 'cols', axis=0, tiled=True)  35.9 us
    another operation x6, other arithmetic, full_path(): lower = jnp.linalg.cholesky(gram)  34.2 us
    ppermute x23, waiting for transfers between devices, swap(): return lax.ppermute(x, axis, [(i, i ^ bit) for i in range(count)])  33.6 us
    another operation x1, loops' own time, full_path(): totals = lax.fori_loop(0, tile_count[0], step, totals)  31.9 us
    ppermute x23, starting transfers between devices, swap(): return lax.ppermute(x, axis, [(i, i ^ bit) for i in range(count)])  28 us
    another operation x5, other arithmetic, full_path(): lax.linalg.triangular_solve(lower, sketch, left_side=False, lower=True, t...  20.6 us
  transfers between devices with their start and end apart: 25, of which 12 were waited for; matrix products, arithmetic and copies ran while one was open for 0% of the time, Pallas kernels for 2%

profile of v2, /device:TPU:2, one launch (start us, length us, event | category | flops | bytes accessed | tf_op | source)
XLA Modules:
  0.0 701.6 jit_solution(6157703329146083224)
XLA Ops:
  6.5 3.4 fusion.22
  10.0 1.3 fusion.20
  11.4 2.1 collective-permute-start.1
  13.6 15.4 %collective-permute-done.1 = f32[264,128]{1,0:T(8,128)S(1)} collective-permute-done((f32[264,128]{1,0:T(8,128)S(1)}, f32[264,128]{1,0:T(8,128)S(1)}, u32[]{:S(2)}, u32[]{:S(2)}) %collective-permute-start.1) | collective-permute-done | bytes 135200 | tf_op jit(solution)/shard_map/ppermute | solution.py:19
  29.0 1.6 collective-permute-start.2
  31.1 3.0 collective-permute-done.2
  34.1 1.6 collective-permute-start.3
  35.8 3.4 collective-permute-done.3
  39.2 2.7 collective-permute-start.4
  43.1 3.5 collective-permute-done.4
  46.7 3.9 shard_map.66
  50.6 4.5 shard_map.67
  55.2 2.5 collective-permute-start.8
  60.3 4.2 shard_map.68
  64.5 1.8 collective-permute-start.17
  67.3 1.2 collective-permute-start.9
  69.5 1.4 collective-permute-done.17
  71.0 2.7 collective-permute-start.18
  74.7 1.0 collective-permute-done.9
  75.7 4.9 collective-permute-start.10
  80.8 3.0 collective-permute-start.19
  84.3 2.8 collective-permute-done.13
  87.8 1.7 collective-permute-done.22
  89.7 605.1 %conditional.1 = (f32[1,1,256,512]{3,2,1,0:T(8,128)}) conditional(s32[]{:T(128)} %bitcast.19, (s32[1]{0:T(128)}, f32[264,128]{1,0:T(8,128)S(1)}, f32[1024,256]{1,0:T(8,128)S(1)}, s32[1,8]{1,0:T(1,128)S(1)}, s32[40]{0:T(128)S(1)}, /*index=5*/s32[40]{0:T(128)S(1)}, bf16[40,512,512]{2,1,0:T(8,128)(2,1)}) %tuple.70, (f32[256,256]{1,0:T(8,128)S(1)}, ...), branch_computations={%region_1.9_spmd, %region_9.10_spmd} | conditional | flops 791134464 | bytes 39858424 | solution.py:259
  90.6 11.7 %cholesky.8 = f32[128,128]{1,0:T(8,128)S(1)} custom-call(f32[128,128]{1,0:T(8,128)S(1)} %cholesky.47), custom_call_target="Cholesky" | custom-call | tf_op jit(solution)/shard_map/cond/branch_0_fun/jit(cholesky)/cholesky | solution.py:188
  102.6 9.8 %custom-call.12 = f32[1,128,128]{1,2,0:T(8,128)S(1)} custom-call(f32[1,128,128]{2,1,0:T(8,128)S(1)} %copy.15), custom_call_target="InvertDiagBlocksLowerTriangular" | custom-call | tf_op jit(solution)/shard_map/cond/branch_0_fun/jit(cholesky)/cholesky | solution.py:188
  113.0 11.7 %cholesky.30 = f32[128,128]{1,0:T(8,128)S(1)} custom-call(f32[128,128]{1,0:T(8,128)S(1)} %convolution_subtract_fusion.1), custom_call_target="Cholesky" | custom-call | tf_op jit(solution)/shard_map/cond/branch_0_fun/jit(cholesky)/cholesky | solution.py:188
  126.9 4.0 while.11
  127.7 1.3 bitcast_dynamic-update-slice_fusion.2
  129.6 1.3 bitcast_dynamic-update-slice_fusion.2
  130.9 19.7 %custom-call.13 = f32[2,128,128]{1,2,0:T(8,128)S(1)} custom-call(f32[2,128,128]{2,1,0:T(8,128)S(1)} %get-tuple-element.107), custom_call_target="InvertDiagBlocksLowerTriangular" | custom-call | tf_op jit(solution)/shard_map/cond/branch_0_fun/triangular_solve | solution.py:189
  151.3 1.0 convolution_subtract_fusion
  153.8 35.9 %all-gather.2.cloned.1.call-done = bf16[4096,256]{0,1:T(8,128)(2,1)} async-done(((bf16[1024,256]{0,1:T(8,128)(2,1)}), bf16[4096,256]{0,1:T(8,128)(2,1)}) %all-gather.2.cloned.1.call-update) | async-done | bytes 2097168 | tf_op jit(solution)/shard_map/cond/branch_0_fun/all_gather | solution.py:190
  189.7 2.5 broadcast.95
  192.2 62.4 %while.10 = (s32[]{:T(128)}, f32[8,256,512]{2,1,0:T(8,128)}, s32[]{:T(128)}, s32[40]{0:T(128)S(1)}, s32[8]{0:T(128)S(1)}, /*index=5*/s32[40]{0:T(128)S(1)}, bf16...) while((s32[]{:T(128)}, f32[8,256,512]{2,1,0:T(8,128)}, ...), condition=%wide.region_7.7_spmd, body=%wide.region_6.6_spmd.sunk | while | flops 134348816 | bytes 2883925 | solution.py:202
  199.2 1.1 constant_dynamic-slice_fusion.4
  200.3 2.2 fusion.37
  209.5 1.1 constant_dynamic-slice_fusion.4
  210.6 2.2 fusion.37
  219.8 1.1 constant_dynamic-slice_fusion.4
  220.9 2.2 fusion.37
  230.1 1.1 constant_dynamic-slice_fusion.4
  231.2 2.2 fusion.37
  240.4 1.1 constant_dynamic-slice_fusion.4
  241.5 2.2 fusion.37
  250.7 1.1 constant_dynamic-slice_fusion.4
  251.8 2.2 fusion.37
  254.7 440.0 %reduce-scatter.2.cloned.1.call-done = f32[1,256,512]{2,1,0:T(8,128)} async-done(((f32[8,256,512]{2,1,0:T(8,128)}), f32[1,256,512]{2,1,0:T(8,128)}) %reduce-scatter.2.cloned.1.call-update) | async-done | bytes 524304 | tf_op jit(solution)/shard_map/cond/branch_0_fun/reduce_scatter | solution.py:203
  (122 shorter events, 23.4 us)
Async XLA Ops:
  10.0 1.4 collective-permute-start
  11.3 19.3 %collective-permute-start.6 = (f32[1024,128]{1,0:T(8,128)S(1)}, f32[1024,128]{1,0:T(8,128)S(1)}, u32[]{:S(2)}, u32[]{:S(2)}) collective-permute-start(f32[1024,128]{1,0:T(8,128)S(1)} %get-tuple-element.152.refs_0_), channel_id=1, source_target_pairs={{0,2},{1,3},{2,0},{3,1},{4,6},{5,7},{6,4},{7,5},{8,10},{9,11},{10,... | collective-permute-start | bytes 1572872 | tf_op jit(solution)/shard_map/ppermute | solution.py:19
  11.4 17.6 %collective-permute-start.1 = (f32[264,128]{1,0:T(8,128)S(1)}, f32[264,128]{1,0:T(8,128)S(1)}, u32[]{:S(2)}, u32[]{:S(2)}) collective-permute-start(f32[264,128]{1,0:T(8,128)S(1)} %fusion.18), channel_id=1, source_target_pairs={{0,2},{1,3},{2,0},{3,1},{4,6},{5,7},{6,4},{7,5},{8,10},{9,11},{10,... | collective-permute-start | bytes 405512 | tf_op jit(solution)/shard_map/ppermute | solution.py:19
  13.5 29.1 %collective-permute-start.15 = (f32[1024,128]{1,0:T(8,128)S(1)}, f32[1024,128]{1,0:T(8,128)S(1)}, u32[]{:S(2)}, u32[]{:S(2)}) collective-permute-start(f32[1024,128]{1,0:T(8,128)S(1)} %get-tuple-element.153.refs_0_), channel_id=1, source_target_pairs={{0,2},{1,3},{2,0},{3,1},{4,6},{5,7},{6,4},{7,5},{8,10},{9,11},{10,... | collective-permute-start | bytes 1572872 | tf_op jit(solution)/shard_map/ppermute | solution.py:19
  29.0 5.1 collective-permute-start.2
  30.6 20.0 %collective-permute-start.5 = (f32[1024,128]{1,0:T(8,128)S(1)}, f32[1024,128]{1,0:T(8,128)S(1)}, u32[]{:S(2)}, u32[]{:S(2)}) collective-permute-start(f32[1024,128]{1,0:T(8,128)S(1)} %get-tuple-element.152.refs_0_), channel_id=1, source_target_pairs={{0,1},{1,0},{2,3},{3,2},{4,5},{5,4},{6,7},{7,6},{8,9},{9,8},{10,11... | collective-permute-start | bytes 1572872 | tf_op jit(solution)/shard_map/ppermute | solution.py:19
  30.6 20.0 %collective-permute-start.7 = (f32[1024,128]{1,0:T(8,128)S(1)}, f32[1024,128]{1,0:T(8,128)}, u32[]{:S(2)}, u32[]{:S(2)}) collective-permute-start(f32[1024,128]{1,0:T(8,128)S(1)} %collective-permute-done.6.refs_2_), channel_id=1, source_target_pairs={{0,1},{1,0},{2,3},{3,2},{4,5},{5,4},{6,7},{7,6},{8,9},{9,8},{10,11... | collective-permute-start | bytes 1572872 | tf_op jit(solution)/shard_map/ppermute | solution.py:19
  34.1 5.1 collective-permute-start.3
  39.2 7.4 %collective-permute-start.4 = (f32[264,128]{1,0:T(8,128)S(1)}, f32[264,128]{1,0:T(8,128)S(1)}, u32[]{:S(2)}, u32[]{:S(2)}) collective-permute-start(f32[264,128]{1,0:T(8,128)S(1)} %add.101), channel_id=1, source_target_pairs={{0,16},{4,20},{8,24},{12,28},{16,0},{20,4},{24,8},{28,12},{1,17},{... | collective-permute-start | bytes 405512 | tf_op jit(solution)/shard_map/ppermute | solution.py:19
  41.9 18.4 %collective-permute-start.14 = (f32[1024,128]{1,0:T(8,128)S(1)}, f32[1024,128]{1,0:T(8,128)S(1)}, u32[]{:S(2)}, u32[]{:S(2)}) collective-permute-start(f32[1024,128]{1,0:T(8,128)S(1)} %get-tuple-element.153.refs_0_), channel_id=1, source_target_pairs={{0,1},{1,0},{2,3},{3,2},{4,5},{5,4},{6,7},{7,6},{8,9},{9,8},{10,11... | collective-permute-start | bytes 1572872 | tf_op jit(solution)/shard_map/ppermute | solution.py:19
  42.6 17.7 %collective-permute-start.16 = (f32[1024,128]{1,0:T(8,128)S(1)}, f32[1024,128]{1,0:T(8,128)S(1)}, u32[]{:S(2)}, u32[]{:S(2)}) collective-permute-start(f32[1024,128]{1,0:T(8,128)S(1)} %collective-permute-done.15.refs_2_), channel_id=1, source_target_pairs={{0,1},{1,0},{2,3},{3,2},{4,5},{5,4},{6,7},{7,6},{8,9},{9,8},{10,11... | collective-permute-start | bytes 1572872 | tf_op jit(solution)/shard_map/ppermute | solution.py:19
  46.7 4.0 copy-start.1
  46.7 4.0 copy-start.2
  46.7 4.0 copy-start.3
  55.2 12.1 %collective-permute-start.8 = (bf16[4,128,256]{2,1,0:T(8,128)(2,1)S(1)}, bf16[4,128,256]{2,1,0:T(8,128)(2,1)S(1)}, u32[]{:S(2)}, u32[]{:S(2)}) collective-permute-start(bf16[4,128,256]{2,1,0:T(8,128)(2,1)S(1)} %get-tuple-element.92), channel_id=1, source_target_pairs={{0,4},{4,0},{8,12},{12,8},{16,20},{20,16},{24,28},{28,24},{1,5},{5... | collective-permute-start | bytes 786440 | tf_op jit(solution)/shard_map/ppermute | solution.py:19
  60.2 8.3 %collective-permute-start.11 = (bf16[4,128,256]{2,1,0:T(8,128)(2,1)S(1)}, bf16[4,128,256]{2,1,0:T(8,128)(2,1)S(1)}, u32[]{:S(2)}, u32[]{:S(2)}) collective-permute-start(bf16[4,128,256]{2,1,0:T(8,128)(2,1)S(1)} %get-tuple-element.94), channel_id=1, source_target_pairs={{0,8},{4,12},{8,0},{12,4},{16,24},{20,28},{24,16},{28,20},{1,9},{5... | collective-permute-start | bytes 786440 | tf_op jit(solution)/shard_map/ppermute | solution.py:19
  64.5 6.4 collective-permute-start.17
  66.3 8.0 %collective-permute-start.20 = (bf16[4,128,256]{2,1,0:T(8,128)(2,1)S(1)}, bf16[4,128,256]{2,1,0:T(8,128)(2,1)S(1)}, u32[]{:S(2)}, u32[]{:S(2)}) collective-permute-start(bf16[4,128,256]{2,1,0:T(8,128)(2,1)S(1)} %get-tuple-element.98), channel_id=1, source_target_pairs={{0,8},{4,12},{8,0},{12,4},{16,24},{20,28},{24,16},{28,20},{1,9},{5... | collective-permute-start | bytes 786440 | tf_op jit(solution)/shard_map/ppermute | solution.py:19
  67.3 8.4 %collective-permute-start.9 = (bf16[2,128,256]{2,1,0:T(8,128)(2,1)S(1)}, bf16[2,128,256]{2,1,0:T(8,128)(2,1)S(1)}, u32[]{:S(2)}, u32[]{:S(2)}) collective-permute-start(bf16[2,128,256]{2,1,0:T(8,128)(2,1)S(1)} %slice.221), channel_id=1, source_target_pairs={{0,8},{4,12},{8,0},{12,4},{16,24},{20,28},{24,16},{28,20},{1,9},{5... | collective-permute-start | bytes 393224 | tf_op jit(solution)/shard_map/ppermute | solution.py:19
  68.6 12.0 %collective-permute-start.12 = (bf16[2,128,256]{2,1,0:T(8,128)(2,1)S(1)}, bf16[2,128,256]{2,1,0:T(8,128)(2,1)S(1)}, u32[]{:S(2)}, u32[]{:S(2)}) collective-permute-start(bf16[2,128,256]{2,1,0:T(8,128)(2,1)S(1)} %slice.220), channel_id=1, source_target_pairs={{0,4},{4,0},{8,12},{12,8},{16,20},{20,16},{24,28},{28,24},{1,5},{5... | collective-permute-start | bytes 393224 | tf_op jit(solution)/shard_map/ppermute | solution.py:19
  70.9 18.7 %copy-start = (f32[1024,256]{1,0:T(8,128)S(1)}, f32[1024,256]{1,0:T(8,128)}, u32[]{:S(2)}) copy-start(f32[1024,256]{1,0:T(8,128)} %param.10) | copy-start | bytes 3145732
  71.0 9.7 %collective-permute-start.18 = (bf16[2,128,256]{2,1,0:T(8,128)(2,1)S(1)}, bf16[2,128,256]{2,1,0:T(8,128)(2,1)S(1)}, u32[]{:S(2)}, u32[]{:S(2)}) collective-permute-start(bf16[2,128,256]{2,1,0:T(8,128)(2,1)S(1)} %slice.219), channel_id=1, source_target_pairs={{0,8},{4,12},{8,0},{12,4},{16,24},{20,28},{24,16},{28,20},{1,9},{5... | collective-permute-start | bytes 393224 | tf_op jit(solution)/shard_map/ppermute | solution.py:19
  74.4 9.4 %collective-permute-start.21 = (bf16[2,128,256]{2,1,0:T(8,128)(2,1)S(1)}, bf16[2,128,256]{2,1,0:T(8,128)(2,1)S(1)}, u32[]{:S(2)}, u32[]{:S(2)}) collective-permute-start(bf16[2,128,256]{2,1,0:T(8,128)(2,1)S(1)} %slice.218), channel_id=1, source_target_pairs={{0,4},{4,0},{8,12},{12,8},{16,20},{20,16},{24,28},{28,24},{1,5},{5... | collective-permute-start | bytes 393224 | tf_op jit(solution)/shard_map/ppermute | solution.py:19
  75.7 8.5 %collective-permute-start.10 = (bf16[1,128,256]{2,1,0:T(8,128)(2,1)S(1)}, bf16[1,128,256]{2,1,0:T(8,128)(2,1)S(1)}, u32[]{:S(2)}, u32[]{:S(2)}) collective-permute-start(bf16[1,128,256]{2,1,0:T(8,128)(2,1)S(1)} %slice.225), channel_id=1, source_target_pairs={{0,16},{4,20},{8,24},{12,28},{16,0},{20,4},{24,8},{28,12},{1,17},{... | collective-permute-start | bytes 196616 | tf_op jit(solution)/shard_map/ppermute | solution.py:19
  80.6 6.5 collective-permute-start.13
  80.8 7.0 %collective-permute-start.19 = (bf16[1,128,256]{2,1,0:T(8,128)(2,1)S(1)}, bf16[1,128,256]{2,1,0:T(8,128)(2,1)S(1)}, u32[]{:S(2)}, u32[]{:S(2)}) collective-permute-start(bf16[1,128,256]{2,1,0:T(8,128)(2,1)S(1)} %slice.223), channel_id=1, source_target_pairs={{0,16},{4,20},{8,24},{12,28},{16,0},{20,4},{24,8},{28,12},{1,17},{... | collective-permute-start | bytes 196616 | tf_op jit(solution)/shard_map/ppermute | solution.py:19
  83.8 5.8 collective-permute-start.22
  89.7 100.0 %all-gather.2.cloned.1.call-start = ((), (), s32[]{:S(2)}) async-start(), calls=%async_computation.1 | async-start | bytes 2621440 | tf_op jit(solution)/shard_map/cond/branch_0_fun/all_gather | solution.py:190
  153.8 540.9 %reduce-scatter.2.cloned.1.call-start = ((), (), s32[]{:S(2)}) async-start(), calls=%async_computation.2 | async-start | bytes 4718592 | tf_op jit(solution)/shard_map/cond/branch_0_fun/reduce_scatter | solution.py:203
Sparse Core Ops, SparseCore 0:
  153.9 35.7 all-gather.1
  254.8 439.8 reduce-scatter.1

commit v3 on v2

v3 whole, which is shorter than its diff:
```python
import functools

import jax
import jax.numpy as jnp
from jax import lax
from jax.experimental import pallas as pl
from jax.experimental.pallas import tpu as pltpu
from jax.sharding import PartitionSpec as P

F32 = jnp.float32
BF16 = jnp.bfloat16
HIGH = lax.Precision.HIGHEST
SLOTS = 12
GROUP = 4
NEAR_COST = 200 * 2**20
FAR_COST = 200 * 2**20
CHUNKS = 2
NEWTON = 2


def bits_of(count):
    return [1 << b for b in reversed(range(count.bit_length() - 1))]


def swap(x, axis, count, bit):
    return lax.ppermute(x, axis, [(i, i ^ bit) for i in range(count)])


def places(order, parity):
    found = [parity << order[0]]
    for bit in reversed(order[1:]):
        found = found + [p | (1 << bit) for p in found]
    return found


def run_tiles(base, span, per_piece, users, items, owner, meta, tiles, slab, add, buf, sems, order):
    count, row, col = meta[0], meta[1], meta[2]

    def relative(t):
        user = users[t]
        return lax.bitwise_xor(user // per_piece, col) - base, lax.rem(user, per_piece)

    def choose(t, n):
        piece, _ = relative(t)
        order[n] = t
        return n + jnp.where((piece >= 0) & (piece < span), 1, 0)

    live = lax.fori_loop(0, count, choose, 0)

    def fetch(i):
        slot = lax.rem(i, SLOTS)
        return pltpu.make_async_copy(tiles.at[order[i]], buf.at[slot], sems.at[slot])

    for i in range(SLOTS):
        @pl.when(i < live)
        def _():
            fetch(i).start()

    def group(first, size):
        for q in range(size):
            fetch(first + q).wait()
        found = []
        for q in range(size):
            piece, part = relative(order[first + q])
            both = jnp.dot(
                slab[piece * per_piece + part],
                buf[lax.rem(first + q, SLOTS)],
                preferred_element_type=F32,
            )
            half = both.shape[0] // 2
            found.append(both[:half] + both[half:])
        for q in range(size):
            add(lax.bitwise_xor(owner[items[order[first + q]]], row), found[q])
        for q in range(size):
            @pl.when(first + q + SLOTS < live)
            def _():
                fetch(first + q + SLOTS).start()

    def finish():
        groups = live // GROUP

        def many(g, _):
            group(g * GROUP, GROUP)
            return 0

        def one(i, _):
            group(i, 1)
            return 0

        lax.fori_loop(0, groups, many, 0)
        lax.fori_loop(groups * GROUP, live, one, 0)

    return finish


def fill(slab, pieces, per_piece):
    tile_size = slab.shape[2]
    kc = slab.shape[1] // 2
    for c, piece in enumerate(pieces):
        for h in range(per_piece):
            block = piece[h * tile_size : (h + 1) * tile_size, :].T
            high = block.astype(BF16)
            slab[c * per_piece + h, :kc, :] = high
            slab[c * per_piece + h, kc:, :] = (block - high.astype(F32)).astype(BF16)


def near_kernel(span, users, items, owner, meta, *refs):
    pieces = refs[:span]
    tiles = refs[span]
    sums = refs[span + 1 : -4]
    slab, buf, sems, order = refs[-4:]
    per_piece = pieces[0].shape[0] // tiles.shape[1]
    kc = sums[0].shape[1]

    def add(place, value):
        for k, part in enumerate(sums):
            part[place] += value[k * kc : (k + 1) * kc]

    finish = run_tiles(
        0, span, per_piece, users, items, owner, meta, tiles, slab, add, buf, sems, order
    )
    for part in sums:
        part[...] = jnp.zeros_like(part)
    fill(slab, pieces, per_piece)
    finish()


def far_kernel(span, orders, users, items, owner, meta, *refs):
    pieces = refs[:span]
    start, tiles = refs[span], refs[span + 1]
    outs = refs[span + 2 : -5]
    slab, buf, sems, order, acc = refs[-5:]
    tile_size = tiles.shape[1]
    per_piece = pieces[0].shape[0] // tile_size

    def add(place, value):
        acc[place] += value

    finish = run_tiles(
        span, span, per_piece, users, items, owner, meta, tiles, slab, add, buf, sems, order
    )
    acc[...] = start[...]
    fill(slab, pieces, per_piece)
    finish()
    width = tile_size // len(orders)
    for o, bits in enumerate(orders):
        cut = slice(o * width, (o + 1) * width)
        for k, place in enumerate(places(bits, 0)):
            outs[2 * o][k] = acc[place, :, cut]
        for k, place in enumerate(places(bits, 1)):
            outs[2 * o + 1][k] = acc[place, :, cut].astype(BF16)


def tile_call(kernel, scalars, pieces, extra, tiles, shapes, scratch, seconds):
    users = scalars[0].shape[0]
    tile_size = tiles.shape[1]
    blocks = len(pieces) * pieces[0].shape[0] // tile_size
    smem = pl.BlockSpec(memory_space=pltpu.SMEM)
    vmem = pl.BlockSpec(memory_space=pltpu.VMEM)
    return pl.pallas_call(
        kernel,
        out_shape=shapes,
        in_specs=[smem] * len(scalars)
        + [vmem] * (len(pieces) + len(extra))
        + [pl.BlockSpec(memory_space=pl.ANY)],
        out_specs=[vmem] * len(shapes),
        scratch_shapes=[
            pltpu.VMEM((blocks, 2 * pieces[0].shape[1], tile_size), BF16),
            pltpu.VMEM((SLOTS, tile_size, tile_size), BF16),
            pltpu.SemaphoreType.DMA((SLOTS,)),
            pltpu.SMEM((users,), jnp.int32),
        ]
        + scratch,
        compiler_params=pltpu.CompilerParams(vmem_limit_bytes=32 * 2**20),
        cost_estimate=pl.CostEstimate(
            flops=0, bytes_accessed=seconds, transcendentals=0
        ),
    )(*scalars, *pieces, *extra, tiles)


def near_sums(scalars, pieces, tiles, rows):
    tile_size = tiles.shape[1]
    kc = pieces[0].shape[1] // CHUNKS
    shapes = [jax.ShapeDtypeStruct((rows, kc, tile_size), F32)] * CHUNKS
    return tile_call(
        functools.partial(near_kernel, len(pieces)), scalars, pieces, [], tiles, shapes, [], NEAR_COST
    )


def far_sums(scalars, pieces, start, tiles, orders):
    rows, kc, tile_size = start.shape
    width = tile_size // len(orders)
    shapes = []
    for _ in orders:
        shapes.append(jax.ShapeDtypeStruct((rows // 2, kc, width), F32))
        shapes.append(jax.ShapeDtypeStruct((rows // 2, kc, width), BF16))
    return tile_call(
        functools.partial(far_kernel, len(pieces), orders),
        scalars,
        pieces,
        [start],
        tiles,
        shapes,
        [pltpu.VMEM(start.shape, F32)],
        FAR_COST,
    )


def mm(a, b):
    return lax.dot_general(a, b, (((1,), (0,)), ((), ())), precision=HIGH, preferred_element_type=F32)


def mmt(a, b):
    return lax.dot_general(a, b, (((1,), (1,)), ((), ())), precision=HIGH, preferred_element_type=F32)


def factor_kernel(packed, inverse, check):
    n = packed.shape[1]
    r = lax.broadcasted_iota(jnp.int32, (n, n), 0)
    c = lax.broadcasted_iota(jnp.int32, (n, n), 1)
    mixed = packed[:n]
    flipped = mixed.T
    side = packed[n : 2 * n]
    tail = jnp.broadcast_to(packed[2 * n : 2 * n + 1], (n, n))
    first = jnp.where(r >= c, mixed, flipped)
    second = jnp.where(r < c, mixed, jnp.where(r > c, flipped, tail))
    gram = jnp.concatenate(
        [jnp.concatenate([first, side.T], axis=1), jnp.concatenate([side, second], axis=1)], axis=0
    )
    m = 2 * n
    rr = lax.broadcasted_iota(jnp.int32, (m, m), 0)
    cc = lax.broadcasted_iota(jnp.int32, (m, m), 1)
    on = rr == cc
    eye = jnp.where(on, 1.0, 0.0).astype(F32)
    low = jnp.where(rr > cc, 1.0, jnp.where(on, 0.5, 0.0)).astype(F32)
    diag = jnp.where(on, gram, 0.0)
    scale_row = lax.rsqrt(jnp.sum(diag, axis=0, keepdims=True))
    scale_col = lax.rsqrt(jnp.sum(diag, axis=1, keepdims=True))
    unit = gram * scale_row * scale_col
    off = unit - eye
    square = jnp.dot(off, off, preferred_element_type=F32)
    spread = jnp.max(jnp.sum(jnp.abs(jnp.dot(square, square, preferred_element_type=F32)), axis=1))
    w = eye - low * off
    for _ in range(NEWTON):
        err = mmt(mm(w, unit), w) - eye
        w = w - mm(low * err, w)
    last = jnp.max(jnp.sum(jnp.abs(err), axis=1))
    inflation = jnp.max(jnp.sum(w * w, axis=0))
    inverse[...] = w * scale_row
    check[0] = spread
    check[1] = last
    check[2] = inflation


def factor(packed):
    n = packed.shape[1]
    return pl.pallas_call(
        factor_kernel,
        out_shape=[jax.ShapeDtypeStruct((2 * n, 2 * n), F32), jax.ShapeDtypeStruct((3,), F32)],
        in_specs=[pl.BlockSpec(memory_space=pltpu.VMEM)],
        out_specs=[pl.BlockSpec(memory_space=pltpu.VMEM), pl.BlockSpec(memory_space=pltpu.SMEM)],
        compiler_params=pltpu.CompilerParams(vmem_limit_bytes=24 * 2**20),
        cost_estimate=pl.CostEstimate(
            flops=11 * 6 * 2 * 8 * n**3, bytes_accessed=6 * 4 * n * n, transcendentals=0
        ),
    )(packed)


def pack(gram):
    n = gram.shape[0] // 2
    r = lax.broadcasted_iota(jnp.int32, (n, n), 0)
    c = lax.broadcasted_iota(jnp.int32, (n, n), 1)
    mixed = jnp.where(r >= c, gram[:n, :n], gram[n:, n:])
    tail = jnp.sum(jnp.where(r == c, gram[n:, n:], 0.0), axis=0, keepdims=True)
    return jnp.concatenate([mixed, gram[n:, :n], jnp.broadcast_to(tail, (8, n))], axis=0)


def full_path(rows, cols, sketch, tiles, tile_user, tile_item, tile_count, item_owner, packed):
    n = packed.shape[1]
    r = lax.broadcasted_iota(jnp.int32, (n, n), 0)
    c = lax.broadcasted_iota(jnp.int32, (n, n), 1)
    mixed, side, tail = packed[:n], packed[n : 2 * n], packed[2 * n : 2 * n + 1]
    first = jnp.where(r >= c, mixed, mixed.T)
    second = jnp.where(r < c, mixed, jnp.where(r > c, mixed.T, tail))
    gram = jnp.block([[first, side.T], [side, second]])
    lower = jnp.linalg.cholesky(gram)
    basis = lax.linalg.triangular_solve(lower, sketch, left_side=False, lower=True, transpose_a=True).astype(BF16)
    have = {0: basis}
    for bit in bits_of(cols):
        for place in list(have):
            have[place | bit] = swap(have[place], "cols", cols, bit)
    slab = jnp.concatenate([have[i] for i in range(cols)], axis=0)
    col = lax.axis_index("cols")
    row = lax.axis_index("rows")
    per_piece = sketch.shape[0] // tiles.shape[2]
    owner = item_owner[0]
    tile_size = tiles.shape[2]

    def step(index, sums):
        user = tile_user[index]
        block = lax.bitwise_xor(user // per_piece, col) * per_piece + user % per_piece
        part_rows = lax.dynamic_slice_in_dim(slab, block * tile_size, tile_size, 0)
        part = lax.dot_general(part_rows, tiles[index], (((0,), (0,)), ((), ())), preferred_element_type=F32)
        place = lax.bitwise_xor(owner[tile_item[index]], row)
        now = lax.dynamic_index_in_dim(sums, place, 0, keepdims=False)
        return lax.dynamic_update_index_in_dim(sums, now + part, place, 0)

    totals = jnp.zeros((owner.shape[0], sketch.shape[1], tile_size), F32)
    totals = lax.fori_loop(0, tile_count[0], step, totals)
    for bit in bits_of(rows):
        totals = totals[:bit] + swap(totals[bit:], "rows", rows, bit)
    return totals[0]


def exchange(keep, send, bit, rows):
    return keep + swap(send, "rows", rows, 1 << bit).astype(F32)


def firsts(outs, orders, rows):
    return [exchange(outs[2 * o], outs[2 * o + 1], order[0], rows) for o, order in enumerate(orders)]


def split(total):
    half = total.shape[0] // 2
    return total[:half], total[half:].astype(BF16)


def body(rows, cols, sketch, tiles, tile_user, tile_item, tile_count, item_owner):
    width = sketch.shape[1]
    row_bits = rows.bit_length() - 1
    first_order = tuple(range(row_bits))
    orders = (first_order, (1, 0) + first_order[2:])
    row = lax.axis_index("rows")
    col = lax.axis_index("cols")
    meta = jnp.stack([tile_count[0], row, col]).astype(jnp.int32)
    scalars = (tile_user, tile_item, item_owner[0], meta)
    kc = width // CHUNKS
    far_bit, *near_bits = bits_of(cols)

    def spread(piece):
        have = {0: piece}
        for bit in near_bits:
            for place in list(have):
                have[place | bit] = swap(have[place], "cols", cols, bit)
        return [have[i] for i in range(cols // 2)]

    fence = lax.optimization_barrier
    crossed = [swap(sketch[:, k * kc : (k + 1) * kc], "cols", cols, far_bit) for k in range(CHUNKS)]
    near = spread(sketch)
    gram = lax.dot_general(
        sketch, sketch, (((0,), (0,)), ((), ())), precision=HIGH, preferred_element_type=F32
    )
    packed = pack(gram)
    for bit in near_bits:
        packed = packed + swap(packed, "cols", cols, bit)
    got = swap(packed, "rows", rows, 1)
    sums = near_sums(scalars, near, tiles, rows)
    crossed[0], packed, got, *sums = fence((crossed[0], packed, got, *sums))
    packed = packed + got
    got = swap(packed, "rows", rows, 2)
    outs = far_sums(scalars, spread(crossed[0]), sums[0], tiles, orders)
    crossed[1], packed, got, *outs = fence((crossed[1], packed, got, *outs))
    packed = packed + got
    got = swap(packed, "rows", rows, 4)
    totals = firsts(outs, orders, rows)
    crossed[1], *totals = fence((crossed[1], *totals))
    halves = [split(t) for t in totals]
    came = [swap(h[1], "rows", rows, 1 << order[1]) for h, order in zip(halves, orders)]
    outs = far_sums(scalars, spread(crossed[1]), sums[1], tiles, orders)
    packed, got, *rest = fence((packed, got, *outs, *[h[0] for h in halves]))
    outs, keeps = rest[: len(outs)], rest[len(outs) :]
    packed = packed + got
    packed = packed + swap(packed, "cols", cols, far_bit)
    for b in range(3, row_bits):
        packed = packed + swap(packed, "rows", rows, 1 << b)
    inverse, check = factor(packed)
    early = [keep + c.astype(F32) for keep, c in zip(keeps, came)]
    late = [exchange(*split(t), order[1], rows) for t, order in zip(firsts(outs, orders, rows), orders)]
    done = []
    for pair in (early, late):
        for pos in range(2, row_bits):
            pair = [exchange(*split(t), order[pos], rows) for t, order in zip(pair, orders)]
        done.append(jnp.concatenate([t[0] for t in pair], axis=1))
    total = jnp.concatenate(done, axis=0)
    good = (check[0] < 0.025) & (check[1] < 0.01) & (check[2] < 1.1)
    out = lax.cond(
        good,
        lambda: mm(inverse, total),
        lambda: full_path(rows, cols, sketch, tiles, tile_user, tile_item, tile_count, item_owner, packed),
    )
    return out[None, None]


def solution(mesh):
    placed = (
        P(("rows", "cols"), None),
        P(("rows", "cols"), None, None),
        P(("rows", "cols")),
        P(("rows", "cols")),
        P(("rows", "cols")),
        P("cols", None),
    )
    return jax.shard_map(
        functools.partial(body, mesh.shape["rows"], mesh.shape["cols"]),
        mesh=mesh,
        in_specs=placed,
        out_specs=P("rows", "cols", None, None),
        check_vma=False,
    )
```

time: 710 us -> 664 us (0.935); the launches traced: 702 us -> 671 us
  waiting for transfers between devices: 510 us -> 91.9 us
  loops' own time: 33.6 us -> 207 us
  local copies, waits for them, and re-layouts: 26.2 us -> 123 us
  matrix products: 19.5 us -> 92.2 us
  starting transfers between devices: 28.3 us -> 67.7 us
  Pallas kernels: 12.6 us -> 27.6 us
  between operations: 16.2 us -> 2.91 us
    reduce_scatter x1 -> x0, waiting for transfers between devices: 440 us -> none  [full_path(): return lax.psum_scatter(totals, 'rows', scatter_dimension=0, tiled=True)[0]]
    another operation x1, loops' own time: 31.9 us -> 205 us  [full_path(): totals = lax.fori_loop(0, tile_count[0], step, totals)]
    dot_general x6 -> x40, matrix products: 13.4 us -> 86.1 us  [step(): lax.dot_general(part_rows, tiles[index], (((0,), (0,)), ((), ())), prefer...]
    ppermute x23 -> x28, waiting for transfers between devices: 33.6 us -> 91.9 us  [swap(): return lax.ppermute(x, axis, [(i, i ^ bit) for i in range(count)])]
    dynamic_slice x18 -> x120, local copies, waits for them, and re-layouts: 10.6 us -> 67.2 us  [the longest x80 44.7 us: step(): place = lax.bitwise_xor(owner[tile_item[index]], row)]
    ppermute x23 -> x28, starting transfers between devices: 28 us -> 67.7 us  [swap(): return lax.ppermute(x, axis, [(i, i ^ bit) for i in range(count)])]
    dynamic_slice x6 -> x40, local copies, waits for them, and re-layouts: 6.5 us -> 43.3 us  [step(): now = lax.dynamic_index_in_dim(sums, place, 0, keepdims=False)]
    all_gather x1 -> x0, waiting for transfers between devices: 35.9 us -> none  [full_path(): slab = lax.all_gather(basis, 'cols', axis=0, tiled=True)]
  transfers between devices with their start and end apart: 25 -> 28, of which waited for: 12 -> 15; matrix products, arithmetic and copies ran while one was open for 0% -> 1% of each run, Pallas kernels for 2% -> 4%
where the time goes in v3:
time: 664 us; the launch traced here: 671 us
  loops' own time  207 us (31%)
  local copies, waits for them, and re-layouts  123 us (19%)
  matrix products  92.2 us (14%)
  waiting for transfers between devices  91.9 us (14%)
  starting transfers between devices  67.7 us (10%)
  other arithmetic  58.5 us (9%)
  Pallas kernels  27.6 us (4%)
    another operation x1, loops' own time, full_path(): totals = lax.fori_loop(0, tile_count[0], step, totals)  205 us
    ppermute x28, waiting for transfers between devices, swap(): return lax.ppermute(x, axis, [(i, i ^ bit) for i in range(count)])  91.9 us
    dot_general x40, matrix products, step(): lax.dot_general(part_rows, tiles[index], (((0,), (0,)), ((), ())), prefer...  86.1 us
    ppermute x28, starting transfers between devices, swap(): return lax.ppermute(x, axis, [(i, i ^ bit) for i in range(count)])  67.7 us
    dynamic_slice x80, local copies, waits for them, and re-layouts, step(): place = lax.bitwise_xor(owner[tile_item[index]], row)  44.7 us
    dynamic_slice x40, local copies, waits for them, and re-layouts, step(): now = lax.dynamic_index_in_dim(sums, place, 0, keepdims=False)  43.3 us
    another operation x6, other arithmetic, full_path(): lower = jnp.linalg.cholesky(gram)  34.1 us
    pallas_call x3, Pallas kernels, tile_call(): pl.pallas_call(kernel, out_shape=shapes, in_specs=[smem] * len(scalars) +...  23.7 us
  transfers between devices with their start and end apart: 28, of which 15 were waited for; matrix products, arithmetic and copies ran while one was open for 1% of the time, Pallas kernels for 4%

profile of v3, /device:TPU:2, one launch (start us, length us, event | category | flops | bytes accessed | tf_op | source)
XLA Modules:
  0.0 671.3 jit_solution(3564348430602040030)
XLA Ops:
  2.2 3.4 fusion.23
  10.0 9.9 %shard_map.66 = (f32[8,128,512]{2,1,0:T(8,128)S(1)}, f32[8,128,512]{2,1,0:T(8,128)S(1)}) custom-call(s32[40]{0:T(128)S(1)} %copy-done.5, s32[40]{0:T(128)S(1)} %copy-done.4, s32[8]{0:T(128)S(1)} %bitcast.88, s32[3]{0:T(128)S(1)} %pad_add_fusion.meta, f32[1024,256]{1,0:T(8,128)S(1)} %copy-done.1, f32[1024,256]{1,0:T(8,128)S(1)} %collective-permute-done.10.refs_1_, ...), custom_call_target="tpu_custom_call" | custom-call | bytes 209715200 | tf_op jit(solution)/shard_map/pallas_call | solution.py:160
  21.9 6.9 %shard_map.67 = (f32[4,128,256]{2,1,0:T(8,128)S(1)}, bf16[4,128,256]{2,1,0:T(8,128)(2,1)S(1)}, f32[4,128,256]{2,1,0:T(8,128)S(1)}, bf16[4,128,256]{2,1,0:T(8,128)(2,1)S(1)}) custom-call(s32[40]{0:T(128)S(1)} %copy-done.5, s32[40]{0:T(128)S(1)} %copy-done.4, s32[8]{0:T(128)S(1)} %bitcast.89, s32[3]{0:T(128)S(1)} %pad_add_fusion.meta, ...), custom_call_target="tpu_custom_call" | custom-call | bytes 209715200 | tf_op jit(solution)/shard_map/pallas_call | solution.py:160
  28.8 5.5 collective-permute-done.6.refs_0_
  34.4 7.9 %collective-permute-done.14 = bf16[4,128,256]{2,1,0:T(8,128)(2,1)S(1)} collective-permute-done((bf16[4,128,256]{2,1,0:T(8,128)(2,1)S(1)}, bf16[4,128,256]{2,1,0:T(8,128)(2,1)S(1)}, u32[]{:S(2)}, u32[]{:S(2)}) %collective-permute-start.14) | collective-permute-done | bytes 262176 | tf_op jit(solution)/shard_map/ppermute | solution.py:26
  46.6 6.9 %shard_map.68 = (f32[4,128,256]{2,1,0:T(8,128)S(1)}, bf16[4,128,256]{2,1,0:T(8,128)(2,1)S(1)}, f32[4,128,256]{2,1,0:T(8,128)S(1)}, bf16[4,128,256]{2,1,0:T(8,128)(2,1)S(1)}) custom-call(s32[40]{0:T(128)S(1)} %copy-done.5, s32[40]{0:T(128)S(1)} %copy-done.4, s32[8]{0:T(128)S(1)} %bitcast.90, s32[3]{0:T(128)S(1)} %pad_add_fusion.meta, ...), custom_call_target="tpu_custom_call" | custom-call | bytes 209715200 | tf_op jit(solution)/shard_map/pallas_call | solution.py:160
  53.7 3.0 collective-permute-start.21
  57.5 2.9 collective-permute-done.19
  61.8 3.9 shard_map.69
  70.1 3.3 collective-permute-done.23
  76.5 3.1 collective-permute-done.24
  80.4 590.1 %conditional.1 = (f32[1,1,256,512]{3,2,1,0:T(8,128)S(1)}) conditional(s32[]{:T(128)} %bitcast.22, (s32[1]{0:T(128)}, f32[264,128]{1,0:T(8,128)S(1)}, f32[1024,256]{1,0:T(8,128)S(1)}, s32[1,8]{1,0:T(1,128)S(1)}, s32[40]{0:T(128)S(1)}, /*index=5*/s32[40]{0:T(128)S(1)}, bf16[40,512,512]{2,1,0:T(8,128)(2,1)}) %tuple.83, (f32[256,256]{1,0:T(8,128)}, ...), branch_computations={%region_1.8_spmd, %region_8.9_spmd} | conditional | flops 802537728 | bytes 78131984 | solution.py:386
  81.3 11.7 %cholesky.8 = f32[128,128]{1,0:T(8,128)S(1)} custom-call(f32[128,128]{1,0:T(8,128)S(1)} %cholesky.47), custom_call_target="Cholesky" | custom-call | tf_op jit(solution)/shard_map/cond/branch_0_fun/jit(cholesky)/cholesky | solution.py:286
  93.4 9.8 %custom-call.12 = f32[1,128,128]{1,2,0:T(8,128)S(1)} custom-call(f32[1,128,128]{2,1,0:T(8,128)S(1)} %copy.15), custom_call_target="InvertDiagBlocksLowerTriangular" | custom-call | tf_op jit(solution)/shard_map/cond/branch_0_fun/jit(cholesky)/cholesky | solution.py:286
  103.7 11.7 %cholesky.30 = f32[128,128]{1,0:T(8,128)S(1)} custom-call(f32[128,128]{1,0:T(8,128)S(1)} %convolution_subtract_fusion.1), custom_call_target="Cholesky" | custom-call | tf_op jit(solution)/shard_map/cond/branch_0_fun/jit(cholesky)/cholesky | solution.py:286
  117.6 3.9 while.13
  121.5 19.7 %custom-call.13 = f32[2,128,128]{1,2,0:T(8,128)S(1)} custom-call(f32[2,128,128]{2,1,0:T(8,128)S(1)} %get-tuple-element.245), custom_call_target="InvertDiagBlocksLowerTriangular" | custom-call | tf_op jit(solution)/shard_map/cond/branch_0_fun/triangular_solve | solution.py:287
  145.0 11.2 %collective-permute-done.1 = bf16[1024,256]{0,1:T(8,128)(2,1)S(1)} collective-permute-done((bf16[1024,256]{0,1:T(8,128)(2,1)S(1)}, bf16[1024,256]{0,1:T(8,128)(2,1)S(1)}, u32[]{:S(2)}, u32[]{:S(2)}) %collective-permute-start.1) | collective-permute-done | bytes 524320 | tf_op jit(solution)/shard_map/cond/branch_0_fun/ppermute | solution.py:26
  158.2 3.1 pad_maximum_fusion
  161.3 2.5 broadcast.97
  163.8 401.5 %while.12 = (s32[]{:T(128)}, f32[8,256,512]{2,1,0:T(8,128)}, s32[]{:T(128)}, s32[40]{0:T(128)S(1)}, s32[8]{0:T(128)S(1)}, /*index=5*/s32[]{:T(128)}, s32[40]{0:T...) while((s32[]{:T(128)}, f32[8,256,512]{2,1,0:T(8,128)}, ...), condition=%wide.region_7.7_spmd, body=%wide.region_6.6_spmd.sunk | while | flops 134348832 | bytes 2884192 | solution.py:309
  171.7 2.2 fusion.38
  221.8 2.2 fusion.38
  231.8 2.2 fusion.38
  241.8 2.2 fusion.38
  251.8 2.2 fusion.38
  271.9 2.2 fusion.38
  281.9 2.2 fusion.38
  291.9 2.1 fusion.38
  312.0 2.2 fusion.38
  352.1 2.2 fusion.38
  382.1 2.2 fusion.38
  392.2 2.2 fusion.38
  402.2 2.2 fusion.38
  412.2 2.2 fusion.38
  432.2 2.2 fusion.38
  442.3 2.2 fusion.38
  462.3 2.2 fusion.38
  472.3 2.2 fusion.38
  482.4 2.2 fusion.38
  492.4 2.1 fusion.38
  502.4 2.2 fusion.38
  512.4 2.2 fusion.38
  522.5 2.2 fusion.38
  567.4 26.9 %collective-permute-done.3 = f32[4,256,512]{2,1,0:T(8,128)S(1)} collective-permute-done((f32[4,256,512]{2,1,0:T(8,128)S(1)}, f32[4,256,512]{2,1,0:T(8,128)S(1)}, u32[]{:S(2)}, u32[]{:S(2)}) %collective-permute-start.3) | collective-permute-done | bytes 2097184 | tf_op jit(solution)/shard_map/cond/branch_0_fun/ppermute | solution.py:26
  594.9 14.8 %collective-permute-done.4 = f32[2,256,512]{2,1,0:T(8,128)S(1)} collective-permute-done((f32[2,256,512]{2,1,0:T(8,128)S(1)}, f32[2,256,512]{2,1,0:T(8,128)S(1)}, u32[]{:S(2)}, u32[]{:S(2)}) %collective-permute-start.4) | collective-permute-done | bytes 1048608 | tf_op jit(solution)/shard_map/cond/branch_0_fun/ppermute | solution.py:26
  610.0 50.7 %collective-permute-start.5 = (f32[1,256,512]{2,1,0:T(8,128)S(1)}, f32[1,256,512]{2,1,0:T(8,128)S(1)}, u32[]{:S(2)}, u32[]{:S(2)}) collective-permute-start(f32[1,256,512]{2,1,0:T(8,128)S(1)} %slice.189), channel_id=1, source_target_pairs={{0,4},{4,0},{8,12},{12,8},{16,20},{20,16},{24,28},{28,24},{1,5},{5... | collective-permute-start | bytes 1572872 | tf_op jit(solution)/shard_map/cond/branch_0_fun/ppermute | solution.py:26
  660.6 9.6 %collective-permute-done.5 = f32[1,256,512]{2,1,0:T(8,128)S(1)} collective-permute-done((f32[1,256,512]{2,1,0:T(8,128)S(1)}, f32[1,256,512]{2,1,0:T(8,128)S(1)}, u32[]{:S(2)}, u32[]{:S(2)}) %collective-permute-start.5) | collective-permute-done | bytes 524320 | tf_op jit(solution)/shard_map/cond/branch_0_fun/ppermute | solution.py:26
  (310 shorter events, 183.5 us)
Async XLA Ops:
  0.0 10.0 %copy-start.1 = (f32[1024,256]{1,0:T(8,128)S(1)}, f32[1024,256]{1,0:T(8,128)}, u32[]{:S(2)}) copy-start(f32[1024,256]{1,0:T(8,128)} %refs_0_.1) | copy-start | bytes 3145732
  0.0 10.0 %copy-start.4 = (s32[40]{0:T(128)S(1)}, s32[40]{0:T(128)}, u32[]{:S(2)}) copy-start(s32[40]{0:T(128)} %items.5) | copy-start | bytes 484
  0.0 10.0 %copy-start.5 = (s32[40]{0:T(128)S(1)}, s32[40]{0:T(128)}, u32[]{:S(2)}) copy-start(s32[40]{0:T(128)} %users.5) | copy-start | bytes 484
  0.0 10.0 %copy-start.3 = (s32[1,8]{1,0:T(1,128)S(1)}, s32[1,8]{1,0:T(1,128)}, u32[]{:S(2)}) copy-start(s32[1,8]{1,0:T(1,128)} %param.15) | copy-start | bytes 100
  0.0 9.9 %collective-permute-start.10 = (f32[1024,256]{1,0:T(8,128)}, f32[1024,256]{1,0:T(8,128)S(1)}, u32[]{:S(2)}, u32[]{:S(2)}) collective-permute-start(f32[1024,256]{1,0:T(8,128)} %refs_0_.1), channel_id=1, source_target_pairs={{0,1},{1,0},{2,3},{3,2},{4,5},{5,4},{6,7},{7,6},{8,9},{9,8},{10,11... | collective-permute-start | bytes 3145736 | tf_op jit(solution)/shard_map/ppermute | solution.py:26
  2.2 17.7 %collective-permute-start.7 = (f32[1024,128]{1,0:T(8,128)}, f32[1024,128]{1,0:T(8,128)S(1)}, u32[]{:S(2)}, u32[]{:S(2)}) collective-permute-start(f32[1024,128]{1,0:T(8,128)} %get-tuple-element.296), channel_id=1, source_target_pairs={{0,2},{1,3},{2,0},{3,1},{4,6},{5,7},{6,4},{7,5},{8,10},{9,11},{10,... | collective-permute-start | bytes 1572872 | tf_op jit(solution)/shard_map/ppermute | solution.py:26
  5.7 1.5 collective-permute-start.8
  7.2 12.8 %collective-permute-start.9 = (f32[264,128]{1,0:T(8,128)S(1)}, f32[264,128]{1,0:T(8,128)S(1)}, u32[]{:S(2)}, u32[]{:S(2)}) collective-permute-start(f32[264,128]{1,0:T(8,128)S(1)} %fusion.19), channel_id=1, source_target_pairs={{0,4},{4,0},{8,12},{12,8},{16,20},{20,16},{24,28},{28,24},{1,5},{5... | collective-permute-start | bytes 405512 | tf_op jit(solution)/shard_map/ppermute | solution.py:26
  19.9 2.0 collective-permute-start.12
  20.0 14.3 %collective-permute-start.6 = (f32[1024,128]{1,0:T(8,128)S(1)}, f32[1024,128]{1,0:T(8,128)S(1)}, u32[]{:S(2)}, u32[]{:S(2)}) collective-permute-start(f32[1024,128]{1,0:T(8,128)S(1)} %get-tuple-element.297), channel_id=1, source_target_pairs={{0,2},{1,3},{2,0},{3,1},{4,6},{5,7},{6,4},{7,5},{8,10},{9,11},{10,... | collective-permute-start | bytes 1572872 | tf_op jit(solution)/shard_map/ppermute | solution.py:26
  20.1 14.2 %collective-permute-start.11 = (f32[264,128]{1,0:T(8,128)S(1)}, f32[264,128]{1,0:T(8,128)S(1)}, u32[]{:S(2)}, u32[]{:S(2)}) collective-permute-start(f32[264,128]{1,0:T(8,128)S(1)} %add.141), channel_id=1, source_target_pairs={{0,8},{4,12},{8,0},{12,4},{16,24},{20,28},{24,16},{28,20},{1,9},{5... | collective-permute-start | bytes 405512 | tf_op jit(solution)/shard_map/ppermute | solution.py:26
  34.4 7.9 %collective-permute-start.14 = (bf16[4,128,256]{2,1,0:T(8,128)(2,1)S(1)}, bf16[4,128,256]{2,1,0:T(8,128)(2,1)S(1)}, u32[]{:S(2)}, u32[]{:S(2)}) collective-permute-start(bf16[4,128,256]{2,1,0:T(8,128)(2,1)S(1)} %get-tuple-element.216), channel_id=1, source_target_pairs={{0,4},{4,0},{8,12},{12,8},{16,20},{20,16},{24,28},{28,24},{1,5},{5... | collective-permute-start | bytes 786440 | tf_op jit(solution)/shard_map/ppermute | solution.py:26
  34.4 7.9 %collective-permute-start.15 = (bf16[4,128,256]{2,1,0:T(8,128)(2,1)S(1)}, bf16[4,128,256]{2,1,0:T(8,128)(2,1)S(1)}, u32[]{:S(2)}, u32[]{:S(2)}) collective-permute-start(bf16[4,128,256]{2,1,0:T(8,128)(2,1)S(1)} %get-tuple-element.218), channel_id=1, source_target_pairs={{0,8},{4,12},{8,0},{12,4},{16,24},{20,28},{24,16},{28,20},{1,9},{5... | collective-permute-start | bytes 786440 | tf_op jit(solution)/shard_map/ppermute | solution.py:26
  42.4 4.2 collective-permute-start.16
  42.5 11.0 %collective-permute-start.13 = (f32[264,128]{1,0:T(8,128)S(1)}, f32[264,128]{1,0:T(8,128)S(1)}, u32[]{:S(2)}, u32[]{:S(2)}) collective-permute-start(f32[264,128]{1,0:T(8,128)S(1)} %add.142), channel_id=1, source_target_pairs={{0,16},{4,20},{8,24},{12,28},{16,0},{20,4},{24,8},{28,12},{1,17},{... | collective-permute-start | bytes 405512 | tf_op jit(solution)/shard_map/ppermute | solution.py:26
  44.5 9.1 %collective-permute-start.18 = (bf16[2,128,256]{2,1,0:T(8,128)(2,1)S(1)}, bf16[2,128,256]{2,1,0:T(8,128)(2,1)S(1)}, u32[]{:S(2)}, u32[]{:S(2)}) collective-permute-start(bf16[2,128,256]{2,1,0:T(8,128)(2,1)S(1)} %slice.244), channel_id=1, source_target_pairs={{0,8},{4,12},{8,0},{12,4},{16,24},{20,28},{24,16},{28,20},{1,9},{5... | collective-permute-start | bytes 393224 | tf_op jit(solution)/shard_map/ppermute | solution.py:26
  46.2 7.5 %collective-permute-start.20 = (bf16[2,128,256]{2,1,0:T(8,128)(2,1)S(1)}, bf16[2,128,256]{2,1,0:T(8,128)(2,1)S(1)}, u32[]{:S(2)}, u32[]{:S(2)}) collective-permute-start(bf16[2,128,256]{2,1,0:T(8,128)(2,1)S(1)} %slice.243), channel_id=1, source_target_pairs={{0,4},{4,0},{8,12},{12,8},{16,20},{20,16},{24,28},{28,24},{1,5},{5... | collective-permute-start | bytes 393224 | tf_op jit(solution)/shard_map/ppermute | solution.py:26
  53.6 6.8 %collective-permute-start.19 = (bf16[1,128,256]{2,1,0:T(8,128)(2,1)S(1)}, bf16[1,128,256]{2,1,0:T(8,128)(2,1)S(1)}, u32[]{:S(2)}, u32[]{:S(2)}) collective-permute-start(bf16[1,128,256]{2,1,0:T(8,128)(2,1)S(1)} %slice.248), channel_id=1, source_target_pairs={{0,16},{4,20},{8,24},{12,28},{16,0},{20,4},{24,8},{28,12},{1,17},{... | collective-permute-start | bytes 196616 | tf_op jit(solution)/shard_map/ppermute | solution.py:26
  53.7 7.8 %collective-permute-start.21 = (bf16[1,128,256]{2,1,0:T(8,128)(2,1)S(1)}, bf16[1,128,256]{2,1,0:T(8,128)(2,1)S(1)}, u32[]{:S(2)}, u32[]{:S(2)}) collective-permute-start(bf16[1,128,256]{2,1,0:T(8,128)(2,1)S(1)} %slice.247), channel_id=1, source_target_pairs={{0,16},{4,20},{8,24},{12,28},{16,0},{20,4},{24,8},{28,12},{1,17},{... | collective-permute-start | bytes 196616 | tf_op jit(solution)/shard_map/ppermute | solution.py:26
  56.7 5.1 collective-permute-start.17
  56.8 11.5 %collective-permute-start.22 = (bf16[4,128,256]{2,1,0:T(8,128)(2,1)S(1)}, bf16[4,128,256]{2,1,0:T(8,128)(2,1)S(1)}, u32[]{:S(2)}, u32[]{:S(2)}) collective-permute-start(bf16[4,128,256]{2,1,0:T(8,128)(2,1)S(1)} %get-tuple-element.234), channel_id=1, source_target_pairs={{0,4},{4,0},{8,12},{12,8},{16,20},{20,16},{24,28},{28,24},{1,5},{5... | collective-permute-start | bytes 786440 | tf_op jit(solution)/shard_map/ppermute | solution.py:26
  57.4 11.0 %collective-permute-start.25 = (bf16[4,128,256]{2,1,0:T(8,128)(2,1)S(1)}, bf16[4,128,256]{2,1,0:T(8,128)(2,1)S(1)}, u32[]{:S(2)}, u32[]{:S(2)}) collective-permute-start(bf16[4,128,256]{2,1,0:T(8,128)(2,1)S(1)} %get-tuple-element.236), channel_id=1, source_target_pairs={{0,8},{4,12},{8,0},{12,4},{16,24},{20,28},{24,16},{28,20},{1,9},{5... | collective-permute-start | bytes 786440 | tf_op jit(solution)/shard_map/ppermute | solution.py:26
  68.4 5.0 collective-permute-start.23
  68.5 6.0 collective-permute-start.26
  73.4 6.2 collective-permute-start.24
  74.6 5.8 collective-permute-start.27
  143.6 12.6 %collective-permute-start.1 = (bf16[1024,256]{0,1:T(8,128)(2,1)S(1)}, bf16[1024,256]{0,1:T(8,128)(2,1)S(1)}, u32[]{:S(2)}, u32[]{:S(2)}) collective-permute-start(bf16[1024,256]{0,1:T(8,128)(2,1)S(1)} %pad_maximum_fusion.1), channel_id=1, source_target_pairs={{0,2},{1,3},{2,0},{3,1},{4,6},{5,7},{6,4},{7,5},{8,10},{9,11},{10,... | collective-permute-start | bytes 1572872 | tf_op jit(solution)/shard_map/cond/branch_0_fun/ppermute | solution.py:26
  145.0 11.2 %collective-permute-start = (bf16[1024,256]{0,1:T(8,128)(2,1)S(1)}, bf16[1024,256]{0,1:T(8,128)(2,1)}, u32[]{:S(2)}, u32[]{:S(2)}) collective-permute-start(bf16[1024,256]{0,1:T(8,128)(2,1)S(1)} %pad_maximum_fusion.1), channel_id=1, source_target_pairs={{0,1},{1,0},{2,3},{3,2},{4,5},{5,4},{6,7},{7,6},{8,9},{9,8},{10,11... | collective-permute-start | bytes 1572872 | tf_op jit(solution)/shard_map/cond/branch_0_fun/ppermute | solution.py:26
  156.2 2.0 collective-permute-start.2
  565.4 28.9 %copy-start = (f32[8,256,512]{2,1,0:T(8,128)S(1)}, f32[8,256,512]{2,1,0:T(8,128)}, u32[]{:S(2)}) copy-start(f32[8,256,512]{2,1,0:T(8,128)} %get-tuple-element.164) | copy-start | bytes 12582916 | tf_op jit(solution)/shard_map/cond
  567.3 27.0 %collective-permute-start.3 = (f32[4,256,512]{2,1,0:T(8,128)S(1)}, f32[4,256,512]{2,1,0:T(8,128)S(1)}, u32[]{:S(2)}, u32[]{:S(2)}) collective-permute-start(f32[4,256,512]{2,1,0:T(8,128)S(1)} %slice.121), channel_id=1, source_target_pairs={{0,16},{4,20},{8,24},{12,28},{16,0},{20,4},{24,8},{28,12},{1,17},{... | collective-permute-start | bytes 6291464 | tf_op jit(solution)/shard_map/cond/branch_0_fun/ppermute | solution.py:26
  594.8 14.9 %collective-permute-start.4 = (f32[2,256,512]{2,1,0:T(8,128)S(1)}, f32[2,256,512]{2,1,0:T(8,128)S(1)}, u32[]{:S(2)}, u32[]{:S(2)}) collective-permute-start(f32[2,256,512]{2,1,0:T(8,128)S(1)} %slice.187), channel_id=1, source_target_pairs={{0,8},{4,12},{8,0},{12,4},{16,24},{20,28},{24,16},{28,20},{1,9},{5... | collective-permute-start | bytes 3145736 | tf_op jit(solution)/shard_map/cond/branch_0_fun/ppermute | solution.py:26
  610.0 60.2 %collective-permute-start.5 = (f32[1,256,512]{2,1,0:T(8,128)S(1)}, f32[1,256,512]{2,1,0:T(8,128)S(1)}, u32[]{:S(2)}, u32[]{:S(2)}) collective-permute-start(f32[1,256,512]{2,1,0:T(8,128)S(1)} %slice.189), channel_id=1, source_target_pairs={{0,4},{4,0},{8,12},{12,8},{16,20},{20,16},{24,28},{28,24},{1,5},{5... | collective-permute-start | bytes 1572872 | tf_op jit(solution)/shard_map/cond/branch_0_fun/ppermute | solution.py:26
  670.5 0.8 copy-start.2
